TPU v7x, 256 devices: a whole 4x4x8 slice. The times are simulated.
256 devices in a mesh: row: 16 (over z, x_hi), col: 16 (over x_lo, y, core).
Axes of the slice: x: 4 (x_hi: 2, x_lo: 2; x = x_hi * 2 + x_lo), y: 4, z: 8, core: 2. Of those that a mesh axis runs over, the one named last changes fastest.
Arguments:
- features: bfloat16 [96, 256, 4096], P(None, 'row', 'col'), may hold values from -6 to 6
- teacher: bfloat16 [1536, 256, 4096], P(None, 'row', 'col'), may hold values from -6 to 6
- conv_in: bfloat16 [9, 96, 96], replicated, may hold values from -0.21875 to 0.21875
- conv_out: bfloat16 [9, 96, 96], replicated, may hold values from -0.21875 to 0.21875
- projector: bfloat16 [96, 1536], replicated, may hold values from -0.625 to 0.625
Outputs:
- grad_conv_in: float32 [9, 96, 96], replicated
- grad_conv_out: float32 [9, 96, 96], replicated
- grad_projector: float32 [96, 1536], replicated
All inputs are finite; a program needn't handle non-finite values.
Results may differ from a plain program's by a relative error of at most 0.0003.
Values may be sent and summed in bfloat16 or wider, within the bound.
A program may use at most 128 MiB of HBM per device.

v0:
```python
import jax
import jax.numpy as jnp
from jax import lax
from jax.sharding import PartitionSpec as P


def padded_2(cells, sides, width):
    for axis, dim in sides:
        count = lax.axis_size(axis)
        ends = count - 1
        head = lax.slice_in_dim(cells, 0, width, axis=dim)
        tail = lax.slice_in_dim(cells, cells.shape[dim] - width, cells.shape[dim], axis=dim)
        cells = jnp.concatenate(
            [
                lax.ppermute(tail, axis, [(i, (i + 1) % count) for i in range(ends)]),
                cells,
                lax.ppermute(head, axis, [((i + 1) % count, i) for i in range(ends)]),
            ],
            axis=dim,
        )
    return cells


def in_blocks(value, dim, devices):
    before, after = (value.shape[:dim], value.shape[dim + 1 :])
    return jnp.moveaxis(value.reshape(*before, devices, -1, *after), dim, 0)


def summed_on_arrival(value, axis, dim):
    devices = lax.axis_size(axis)
    parts = lax.all_to_all(in_blocks(value, dim, devices), axis, 0, 0, tiled=True)
    return jnp.sum(parts, axis=0)


def in_one_piece(arrays, axis, dim, along):
    ends, at = ([], 0)
    for a in arrays[:-1]:
        at += a.shape[along]
        ends.append(at)
    both = jnp.concatenate(arrays, axis=along)
    return tuple(jnp.split(summed_on_arrival(both, axis, dim), ends, axis=along))


def from_everyone(value, axis):
    devices = lax.axis_size(axis)
    return lax.all_to_all(
        jnp.broadcast_to(value[None], (devices, *value.shape)), axis, 0, 0, tiled=True
    )


def of_everyone(value, axis):
    return from_everyone(value, axis).sum(axis=0)


def in_one(arrays, axis):
    ends = [0]
    for a in arrays:
        ends.append(ends[-1] + a.size)
    so_far = of_everyone(jnp.concatenate([a.ravel() for a in arrays]), axis)
    return tuple((so_far[b:e].reshape(a.shape) for a, b, e in zip(arrays, ends, ends[1:])))


def in_one_piece_2(arrays, axis, dim, along):
    widths = [a.shape[along] for a in arrays]
    both = jnp.concatenate(arrays, axis=along)
    result = lax.all_gather(both, axis, axis=dim, tiled=True)
    return tuple(jnp.split(result, [sum(widths[:k]) for k in range(1, len(widths))], axis=along))


def gelu_grad(value):
    cdf = 0.5 * (1.0 + jax.scipy.special.erf(value * 0.7071067811865476))
    dens = jnp.exp(-0.5 * value * value) * 0.3989422804014327
    return cdf + value * dens


def tap_stack(padded, height, width):
    return jnp.concatenate(
        [padded[:, tap // 3 : tap // 3 + height, tap % 3 : tap % 3 + width] for tap in range(9)], 0
    )


def flip_stack(padded, height, width):
    return jnp.concatenate(
        [
            padded[:, 2 - tap // 3 : 2 - tap // 3 + height, 2 - tap % 3 : 2 - tap % 3 + width]
            for tap in range(9)
        ],
        0,
    )


def shards(features, teacher, conv_in, conv_out, projector):
    chans, height, width = features.shape
    flat_in = conv_in.reshape(9 * chans, chans)
    flat_out = conv_out.reshape(9 * chans, chans)
    xpad = padded_2(features, (("row", 1), ("col", 2)), 1)
    x_taps = tap_stack(xpad, height, width)
    pre = jnp.einsum("ko,khw->ohw", flat_in, x_taps, preferred_element_type=jnp.float32)
    hidden = jax.nn.gelu(pre, approximate=False).astype(jnp.bfloat16)
    gpad = padded_2(hidden, (("row", 1), ("col", 2)), 1)
    g_taps = tap_stack(gpad, height, width)
    branch = jnp.einsum("ko,khw->ohw", flat_out, g_taps, preferred_element_type=jnp.float32)
    student = (features.astype(jnp.float32) + branch).astype(jnp.bfloat16)
    pred = jnp.einsum("ce,chw->ehw", projector, student, preferred_element_type=jnp.float32)
    npix = height * width * lax.axis_size("row") * lax.axis_size("col")
    dpred = ((pred - teacher.astype(jnp.float32)) / npix).astype(jnp.bfloat16)
    grad_proj = jnp.einsum("chw,ehw->ce", student, dpred, preferred_element_type=jnp.float32)
    dstudent = jnp.einsum(
        "ce,ehw->chw", projector, dpred, preferred_element_type=jnp.float32
    ).astype(jnp.bfloat16)
    spad = padded_2(dstudent, (("row", 1), ("col", 2)), 1)
    back_matrix = jnp.transpose(conv_out, (0, 2, 1)).reshape(9 * chans, chans)
    dhidden = jnp.einsum(
        "kc,khw->chw",
        back_matrix,
        flip_stack(spad, height, width),
        preferred_element_type=jnp.float32,
    )
    dpre = (dhidden * gelu_grad(pre)).astype(jnp.bfloat16)
    grad_out = jnp.einsum(
        "khw,ohw->ko", g_taps, dstudent, preferred_element_type=jnp.float32
    ).reshape(9, chans, chans)
    grad_in = jnp.einsum("khw,ohw->ko", x_taps, dpre, preferred_element_type=jnp.float32).reshape(
        9, chans, chans
    )
    owned = (
        *in_one_piece((grad_in, grad_out), "col", 1, 0),
        summed_on_arrival(grad_proj, "col", 1),
    )
    rowed = in_one((owned[0], owned[1], owned[2]), "row")
    result = (
        *in_one_piece_2((rowed[0], rowed[1]), "col", 1, 0),
        lax.all_gather(rowed[2], "col", axis=1, tiled=True),
    )
    return (result[0], result[1], result[2])


def solution(mesh):
    in_specs = (P(None, "row", "col"), P(None, "row", "col"), P(), P(), P())
    out_specs = (P(), P(), P())
    return jax.shard_map(shards, mesh=mesh, in_specs=in_specs, out_specs=out_specs, check_vma=False)
```

profile of v0, /device:TPU:1, one launch (start us, length us, event | category | flops | bytes accessed | tf_op | source)
XLA Modules:
  0.0 258.9 jit_solution(2869301798991492329)
XLA Ops:
  0.7 1.5 copy.102
  2.1 5.5 %collective-permute-start = (bf16[96,1,256]{2,0,1:T(8,128)(2,1)S(1)}, bf16[96,1,256]{2,0,1:T(8,128)(2,1)S(1)}, u32[]{:S(2)}, u32[]{:S(2)}) collective-permute-start(bf16[96,1,256]{2,0,1:T(8,128)(2,1)S(1)} %get-tuple-element.32), channel_id=1, source_target_pairs={{0,16},{16,32},{32,48},{48,64},{64,80},{80,96},{96,112},{112,128},... | collective-permute-start | bytes 147464 | tf_op jit(solution)/shard_map/ppermute | solution.py:15
  7.6 1.3 collective-permute-start.1
  9.2 4.8 %collective-permute-done.1 = bf16[96,1,256]{2,0,1:T(8,128)(2,1)S(1)} collective-permute-done((bf16[96,1,256]{2,0,1:T(8,128)(2,1)S(1)}, bf16[96,1,256]{2,0,1:T(8,128)(2,1)S(1)}, u32[]{:S(2)}, u32[]{:S(2)}) %collective-permute-start.1) | collective-permute-done | bytes 49184 | tf_op jit(solution)/shard_map/ppermute | solution.py:17
  14.2 5.2 %collective-permute-start.2 = (bf16[96,18,1]{2,0,1:T(8,128)(2,1)S(1)}, bf16[96,18,1]{2,0,1:T(8,128)(2,1)S(1)}, u32[]{:S(2)}, u32[]{:S(2)}) collective-permute-start(bf16[96,18,1]{2,0,1:T(8,128)(2,1)S(1)} %get-tuple-element.26), channel_id=1, source_target_pairs={{0,1},{1,2},{2,3},{3,4},{4,5},{5,6},{6,7},{7,8},{8,9},{9,10},{10,1... | collective-permute-start | bytes 10376 | tf_op jit(solution)/shard_map/ppermute | solution.py:15
  19.4 1.9 collective-permute-start.3
  21.3 3.3 %collective-permute-done.2 = bf16[96,18,1]{2,0,1:T(8,128)(2,1)S(1)} collective-permute-done((bf16[96,18,1]{2,0,1:T(8,128)(2,1)S(1)}, bf16[96,18,1]{2,0,1:T(8,128)(2,1)S(1)}, u32[]{:S(2)}, u32[]{:S(2)}) %collective-permute-start.2) | collective-permute-done | bytes 3488 | tf_op jit(solution)/shard_map/ppermute | solution.py:15
  25.0 4.0 %collective-permute-done.3 = bf16[96,18,1]{2,0,1:T(8,128)(2,1)S(1)} collective-permute-done((bf16[96,18,1]{2,0,1:T(8,128)(2,1)S(1)}, bf16[96,18,1]{2,0,1:T(8,128)(2,1)S(1)}, u32[]{:S(2)}, u32[]{:S(2)}) %collective-permute-start.3) | collective-permute-done | bytes 3488 | tf_op jit(solution)/shard_map/ppermute | solution.py:17
  29.0 0.4 fusion.30
  31.0 0.4 fusion.39
  31.8 5.5 %fusion.4 = (bf16[96,16,256]{2,0,1:T(8,128)(2,1)S(1)}, f32[16,256,96]{1,2,0:T(8,128)}) fusion(bf16[864,16,256]{2,0,1:T(8,128)(2,1)S(1)} %fusion.39, bf16[864,96,1]{1,0,2:T(8,128)(2,1)S(1)} %bitcast.109), kind=kOutput, calls=%fused_computation.12 | convolution fusion | flops 705036288 | bytes 9603072 | tf_op jit(solution)/shard_map/ko,khw->ohw/dot_general | solution.py:98
  37.4 4.4 %collective-permute-start.4 = (bf16[96,1,256]{2,0,1:T(8,128)(2,1)S(1)}, bf16[96,1,256]{2,0,1:T(8,128)(2,1)S(1)}, u32[]{:S(2)}, u32[]{:S(2)}) collective-permute-start(bf16[96,1,256]{2,0,1:T(8,128)(2,1)S(1)} %get-tuple-element.29), channel_id=1, source_target_pairs={{0,16},{16,32},{32,48},{48,64},{64,80},{80,96},{96,112},{112,128},... | collective-permute-start | bytes 147464 | tf_op jit(solution)/shard_map/ppermute | solution.py:15
  41.8 1.4 collective-permute-start.5
  43.3 5.0 %collective-permute-done.5 = bf16[96,1,256]{2,0,1:T(8,128)(2,1)S(1)} collective-permute-done((bf16[96,1,256]{2,0,1:T(8,128)(2,1)S(1)}, bf16[96,1,256]{2,0,1:T(8,128)(2,1)S(1)}, u32[]{:S(2)}, u32[]{:S(2)}) %collective-permute-start.5) | collective-permute-done | bytes 49184 | tf_op jit(solution)/shard_map/ppermute | solution.py:17
  48.4 1.0 fusion.52
  49.4 1.9 collective-permute-start.7
  51.3 3.8 %collective-permute-start.6 = (bf16[96,18,1]{2,0,1:T(8,128)(2,1)S(1)}, bf16[96,18,1]{2,0,1:T(8,128)(2,1)S(1)}, u32[]{:S(2)}, u32[]{:S(2)}) collective-permute-start(bf16[96,18,1]{2,0,1:T(8,128)(2,1)S(1)} %get-tuple-element.24), channel_id=1, source_target_pairs={{0,1},{1,2},{2,3},{3,4},{4,5},{5,6},{6,7},{7,8},{8,9},{9,10},{10,1... | collective-permute-start | bytes 10376 | tf_op jit(solution)/shard_map/ppermute | solution.py:15
  55.1 0.8 copy.113
  56.0 16.9 %copy.111 = bf16[1536,16,256]{0,2,1:T(8,128)(2,1)} copy(bf16[1536,16,256]{2,1,0:T(8,128)(2,1)} %param.6) | data formatting | bytes 25165824 | tf_op args[1]
  72.8 1.0 pad_maximum_fusion
  75.4 2.9 %copy-done.2 = bf16[864,16,256]{2,0,1:T(8,128)(2,1)} copy-done((bf16[864,16,256]{2,0,1:T(8,128)(2,1)}, bf16[864,16,256]{2,0,1:T(8,128)(2,1)S(1)}, u32[]{:S(2)}) %copy-start.2) | copy-done | bytes 7077912
  78.3 1.5 fusion.11
  79.8 9.2 %fusion.1 = bf16[1536,16,256]{0,2,1:T(8,128)(2,1)} fusion(bf16[1536,16,256]{0,2,1:T(8,128)(2,1)} %copy.111, bf16[96,16,256]{2,0,1:T(8,128)(2,1)S(1)} %fusion.11, bf16[96,1536]{1,0:T(8,128)(2,1)S(1)} %copy-done), kind=kOutput, calls=%fused_computation.2 | convolution fusion | flops 1233125376 | bytes 26247168 | tf_op jit(solution)/shard_map/ce,chw->ehw/dot_general | solution.py:104
  89.0 8.6 %fusion.26 = bf16[96,16,256]{2,0,1:T(8,128)(2,1)S(1)} fusion(bf16[1536,16,256]{0,2,1:T(8,128)(2,1)} %fusion.1, bf16[96,1536]{1,0:T(8,128)(2,1)S(1)} %copy-done), kind=kOutput, calls=%fused_computation.53 | convolution fusion | flops 1208352768 | bytes 13664256 | tf_op jit(solution)/shard_map/ce,ehw->chw/dot_general | solution.py:108
  97.6 4.6 %collective-permute-start.8 = (bf16[96,1,256]{2,0,1:T(8,128)(2,1)S(1)}, bf16[96,1,256]{2,0,1:T(8,128)(2,1)S(1)}, u32[]{:S(2)}, u32[]{:S(2)}) collective-permute-start(bf16[96,1,256]{2,0,1:T(8,128)(2,1)S(1)} %get-tuple-element.27), channel_id=1, source_target_pairs={{0,16},{16,32},{32,48},{48,64},{64,80},{80,96},{96,112},{112,128},... | collective-permute-start | bytes 147464 | tf_op jit(solution)/shard_map/ppermute | solution.py:15
  102.3 1.6 collective-permute-start.9
  103.9 2.1 convolution_bitcast_fusion
  106.0 3.0 %collective-permute-done.9 = bf16[96,1,256]{2,0,1:T(8,128)(2,1)S(1)} collective-permute-done((bf16[96,1,256]{2,0,1:T(8,128)(2,1)S(1)}, bf16[96,1,256]{2,0,1:T(8,128)(2,1)S(1)}, u32[]{:S(2)}, u32[]{:S(2)}) %collective-permute-start.9) | collective-permute-done | bytes 49184 | tf_op jit(solution)/shard_map/ppermute | solution.py:17
  109.1 1.1 fusion.51
  110.2 3.4 %collective-permute-start.11 = (bf16[96,18,1]{2,0,1:T(8,128)(2,1)}, bf16[96,18,1]{2,0,1:T(8,128)(2,1)}, u32[]{:S(2)}, u32[]{:S(2)}) collective-permute-start(bf16[96,18,1]{2,0,1:T(8,128)(2,1)} %get-tuple-element.19), channel_id=1, source_target_pairs={{0,1},{1,2},{2,3},{3,4},{4,5},{5,6},{6,7},{7,8},{8,9},{9,10},{10,1... | collective-permute-start | bytes 10376 | tf_op jit(solution)/shard_map/ppermute | solution.py:15
  113.6 1.9 collective-permute-start.10
  115.6 2.0 convolution_bitcast_fusion.1
  117.9 1.1 copy.146
  119.0 8.6 %all-to-all-start.1 = ((f32[16,96,96]{2,1,0:T(8,128)}), f32[16,96,96]{2,1,0:T(8,128)S(1)}, u32[]{:S(2)}, u32[]{:S(2)}) async-start(f32[16,96,96]{2,1,0:T(8,128)} %bitcast.103), calls=%async_computation.1 | async-start | bytes 1572864 | tf_op jit(solution)/shard_map/all_to_all | solution.py:31
  127.7 2.1 maximum_maximum_fusion.1
  131.3 2.9 %copy-done.7 = bf16[864,16,256]{2,0,1:T(8,128)(2,1)} copy-done((bf16[864,16,256]{2,0,1:T(8,128)(2,1)}, bf16[864,16,256]{2,0,1:T(8,128)(2,1)S(1)}, u32[]{:S(2)}) %copy-start.7) | copy-done | bytes 7077912
  134.1 8.8 %convolution_bitcast_fusion.2 = f32[864,96]{1,0:T(8,128)S(1)} fusion(bf16[864,16,256]{2,0,1:T(8,128)(2,1)} %copy-done.6, f32[16,256,96]{1,2,0:T(8,128)} %get-tuple-element.38, bf16[864,16,256]{2,0,1:T(8,128)(2,1)} %copy-done.7, bf16[864,96,1]{1,0,2:T(8,128)(2,1)S(1)} %bitcast.108), kind=kOutput, calls=%fused_computation.55 | convolution fusion | flops 1362886656 | bytes 16226304 | tf_op jit(solution)/shard_map/khw,ohw->ko/dot_general | solution.py:123
  143.1 1.1 copy.117
  144.2 5.7 %all-to-all-start = ((f32[16,18,6,96]{3,2,1,0:T(8,128)}), f32[16,18,6,96]{3,2,1,0:T(8,128)S(1)}, u32[]{:S(2)}, u32[]{:S(2)}) async-start(f32[16,18,6,96]{3,2,1,0:T(8,128)} %copy.117), calls=%async_computation | async-start | bytes 2359296 | tf_op jit(solution)/shard_map/all_to_all | solution.py:31
  150.1 17.0 %all-to-all-done = f32[16,18,6,96]{3,2,1,0:T(8,128)S(1)} async-done(((f32[16,18,6,96]{3,2,1,0:T(8,128)}), f32[16,18,6,96]{3,2,1,0:T(8,128)S(1)}, u32[]{:S(2)}, u32[]{:S(2)}) %all-to-all-start) | async-done | bytes 663584 | tf_op jit(solution)/shard_map/all_to_all | solution.py:31
  167.4 0.6 broadcast_in_dim.2
  168.1 44.9 %all_to_all.16 = f32[16,1,19584]{2,1,0:T(1,128)S(1)} all-to-all(f32[16,1,19584]{2,1,0:T(1,128)S(1)} %broadcast_in_dim.2), channel_id=1, replica_groups=mesh['row'=16,'col'=16] {'row'}, dimensions={0} | all-to-all | bytes 2506752 | tf_op jit(solution)/shard_map/all_to_all | solution.py:46
  213.0 0.8 reduce_sum.29
  214.3 21.9 %all_gather.7 = f32[96,1536]{0,1:T(8,128)S(1)} all-gather(f32[96,96]{0,1:T(8,128)S(1)} %copy.122), channel_id=1, replica_groups=mesh['row'=16,'col'=16] {'col'}, dimensions={1}, use_global_device_ids=true | all-gather | bytes 626688 | tf_op jit(solution)/shard_map/all_gather | solution.py:133
  236.2 1.1 copy.125
  237.3 19.8 %all_gather.6 = f32[18,96,96]{2,0,1:T(8,128)S(1)} all-gather(f32[18,6,96]{2,0,1:T(8,128)S(1)} %copy.121), channel_id=1, replica_groups=mesh['row'=16,'col'=16] {'col'}, dimensions={1}, use_global_device_ids=true | all-gather | bytes 705024 | tf_op jit(solution)/shard_map/all_gather | solution.py:66
  257.1 0.9 copy.124
  258.0 0.9 copy.123
  (83 shorter events, 7.6 us)
Async XLA Ops:
  0.6 79.2 %copy-start = (bf16[96,1536]{1,0:T(8,128)(2,1)S(1)}, bf16[96,1536]{1,0:T(8,128)(2,1)}, u32[]{:S(2)}) copy-start(bf16[96,1536]{1,0:T(8,128)(2,1)} %param.9) | copy-start | bytes 884740
  0.6 8.3 %copy-start.3 = (bf16[96,16,256]{2,1,0:T(8,128)(2,1)S(1)}, bf16[96,16,256]{2,1,0:T(8,128)(2,1)}, u32[]{:S(2)}) copy-start(bf16[96,16,256]{2,1,0:T(8,128)(2,1)} %param.5) | copy-start | bytes 2359300
  2.1 6.8 %collective-permute-start = (bf16[96,1,256]{2,0,1:T(8,128)(2,1)S(1)}, bf16[96,1,256]{2,0,1:T(8,128)(2,1)S(1)}, u32[]{:S(2)}, u32[]{:S(2)}) collective-permute-start(bf16[96,1,256]{2,0,1:T(8,128)(2,1)S(1)} %get-tuple-element.32), channel_id=1, source_target_pairs={{0,16},{16,32},{32,48},{48,64},{64,80},{80,96},{96,112},{112,128},... | collective-permute-start | bytes 147464 | tf_op jit(solution)/shard_map/ppermute | solution.py:15
  7.6 6.3 %collective-permute-start.1 = (bf16[96,1,256]{2,0,1:T(8,128)(2,1)S(1)}, bf16[96,1,256]{2,0,1:T(8,128)(2,1)S(1)}, u32[]{:S(2)}, u32[]{:S(2)}) collective-permute-start(bf16[96,1,256]{2,0,1:T(8,128)(2,1)S(1)} %get-tuple-element.31), channel_id=1, source_target_pairs={{16,0},{32,16},{48,32},{64,48},{80,64},{96,80},{112,96},{128,112},... | collective-permute-start | bytes 147464 | tf_op jit(solution)/shard_map/ppermute | solution.py:17
  14.2 10.4 %collective-permute-start.2 = (bf16[96,18,1]{2,0,1:T(8,128)(2,1)S(1)}, bf16[96,18,1]{2,0,1:T(8,128)(2,1)S(1)}, u32[]{:S(2)}, u32[]{:S(2)}) collective-permute-start(bf16[96,18,1]{2,0,1:T(8,128)(2,1)S(1)} %get-tuple-element.26), channel_id=1, source_target_pairs={{0,1},{1,2},{2,3},{3,4},{4,5},{5,6},{6,7},{7,8},{8,9},{9,10},{10,1... | collective-permute-start | bytes 10376 | tf_op jit(solution)/shard_map/ppermute | solution.py:15
  19.4 9.6 %collective-permute-start.3 = (bf16[96,18,1]{2,0,1:T(8,128)(2,1)S(1)}, bf16[96,18,1]{2,0,1:T(8,128)(2,1)S(1)}, u32[]{:S(2)}, u32[]{:S(2)}) collective-permute-start(bf16[96,18,1]{2,0,1:T(8,128)(2,1)S(1)} %get-tuple-element.25), channel_id=1, source_target_pairs={{1,0},{2,1},{3,2},{4,3},{5,4},{6,5},{7,6},{8,7},{9,8},{10,9},{11,1... | collective-permute-start | bytes 10376 | tf_op jit(solution)/shard_map/ppermute | solution.py:17
  30.9 0.9 copy-start.8
  31.4 6.0 %copy-start.6 = (bf16[864,16,256]{2,0,1:T(8,128)(2,1)}, bf16[864,16,256]{2,0,1:T(8,128)(2,1)S(1)}, u32[]{:S(2)}) copy-start(bf16[864,16,256]{2,0,1:T(8,128)(2,1)S(1)} %fusion.39) | copy-start | bytes 21233668
  37.4 5.8 %collective-permute-start.4 = (bf16[96,1,256]{2,0,1:T(8,128)(2,1)S(1)}, bf16[96,1,256]{2,0,1:T(8,128)(2,1)S(1)}, u32[]{:S(2)}, u32[]{:S(2)}) collective-permute-start(bf16[96,1,256]{2,0,1:T(8,128)(2,1)S(1)} %get-tuple-element.29), channel_id=1, source_target_pairs={{0,16},{16,32},{32,48},{48,64},{64,80},{80,96},{96,112},{112,128},... | collective-permute-start | bytes 147464 | tf_op jit(solution)/shard_map/ppermute | solution.py:15
  41.8 13.3 %copy-start.4 = (bf16[9,96,96]{2,1,0:T(8,128)(2,1)S(1)}, bf16[9,96,96]{2,1,0:T(8,128)(2,1)}, u32[]{:S(2)}) copy-start(bf16[9,96,96]{2,1,0:T(8,128)(2,1)} %param.8) | copy-start | bytes 497668
  41.8 6.5 %collective-permute-start.5 = (bf16[96,1,256]{2,0,1:T(8,128)(2,1)S(1)}, bf16[96,1,256]{2,0,1:T(8,128)(2,1)S(1)}, u32[]{:S(2)}, u32[]{:S(2)}) collective-permute-start(bf16[96,1,256]{2,0,1:T(8,128)(2,1)S(1)} %get-tuple-element.30), channel_id=1, source_target_pairs={{16,0},{32,16},{48,32},{64,48},{80,64},{96,80},{112,96},{128,112},... | collective-permute-start | bytes 147464 | tf_op jit(solution)/shard_map/ppermute | solution.py:17
  49.4 23.5 %collective-permute-start.7 = (bf16[96,18,1]{2,0,1:T(8,128)(2,1)}, bf16[96,18,1]{2,0,1:T(8,128)(2,1)S(1)}, u32[]{:S(2)}, u32[]{:S(2)}) collective-permute-start(bf16[96,18,1]{2,0,1:T(8,128)(2,1)} %get-tuple-element.23), channel_id=1, source_target_pairs={{1,0},{2,1},{3,2},{4,3},{5,4},{6,5},{7,6},{8,7},{9,8},{10,9},{11,1... | collective-permute-start | bytes 10376 | tf_op jit(solution)/shard_map/ppermute | solution.py:17
  51.3 21.5 %collective-permute-start.6 = (bf16[96,18,1]{2,0,1:T(8,128)(2,1)S(1)}, bf16[96,18,1]{2,0,1:T(8,128)(2,1)S(1)}, u32[]{:S(2)}, u32[]{:S(2)}) collective-permute-start(bf16[96,18,1]{2,0,1:T(8,128)(2,1)S(1)} %get-tuple-element.24), channel_id=1, source_target_pairs={{0,1},{1,2},{2,3},{3,4},{4,5},{5,6},{6,7},{7,8},{8,9},{9,10},{10,1... | collective-permute-start | bytes 10376 | tf_op jit(solution)/shard_map/ppermute | solution.py:15
  75.4 2.9 %copy-start.2 = (bf16[864,16,256]{2,0,1:T(8,128)(2,1)}, bf16[864,16,256]{2,0,1:T(8,128)(2,1)S(1)}, u32[]{:S(2)}) copy-start(bf16[864,16,256]{2,0,1:T(8,128)(2,1)S(1)} %slice_dynamic-update-slice_fusion.6) | copy-start | bytes 21233668
  89.0 14.9 %copy-start.1 = (bf16[1536,16,256]{0,2,1:T(8,128)(2,1)S(1)}, bf16[1536,16,256]{0,2,1:T(8,128)(2,1)}, u32[]{:S(2)}) copy-start(bf16[1536,16,256]{0,2,1:T(8,128)(2,1)} %fusion.1) | copy-start | bytes 37748740
  97.6 8.4 %collective-permute-start.8 = (bf16[96,1,256]{2,0,1:T(8,128)(2,1)S(1)}, bf16[96,1,256]{2,0,1:T(8,128)(2,1)S(1)}, u32[]{:S(2)}, u32[]{:S(2)}) collective-permute-start(bf16[96,1,256]{2,0,1:T(8,128)(2,1)S(1)} %get-tuple-element.27), channel_id=1, source_target_pairs={{0,16},{16,32},{32,48},{48,64},{64,80},{80,96},{96,112},{112,128},... | collective-permute-start | bytes 147464 | tf_op jit(solution)/shard_map/ppermute | solution.py:15
  102.3 13.2 %slice-start = ((s8[7077888]{0:T(1024)(128)(4,1)}), s8[4194304]{0:T(1024)(128)(4,1)S(1)}, s32[]{:S(2)}) async-start(s8[7077888]{0:T(1024)(128)(4,1)} %bitcast.104), calls=%async_computation.3 | async-start | bytes 8388608
  102.3 13.2 %slice-start.1 = ((s8[7077888]{0:T(1024)(128)(4,1)}), s8[2883584]{0:T(1024)(128)(4,1)S(1)}, s32[]{:S(2)}) async-start(s8[7077888]{0:T(1024)(128)(4,1)} %bitcast.104), calls=%async_computation.4 | async-start | bytes 5767168
  102.3 6.7 %collective-permute-start.9 = (bf16[96,1,256]{2,0,1:T(8,128)(2,1)S(1)}, bf16[96,1,256]{2,0,1:T(8,128)(2,1)S(1)}, u32[]{:S(2)}, u32[]{:S(2)}) collective-permute-start(bf16[96,1,256]{2,0,1:T(8,128)(2,1)S(1)} %get-tuple-element.28), channel_id=1, source_target_pairs={{16,0},{32,16},{48,32},{64,48},{80,64},{96,80},{112,96},{128,112},... | collective-permute-start | bytes 147464 | tf_op jit(solution)/shard_map/ppermute | solution.py:17
  110.2 17.4 %collective-permute-start.11 = (bf16[96,18,1]{2,0,1:T(8,128)(2,1)}, bf16[96,18,1]{2,0,1:T(8,128)(2,1)}, u32[]{:S(2)}, u32[]{:S(2)}) collective-permute-start(bf16[96,18,1]{2,0,1:T(8,128)(2,1)} %get-tuple-element.19), channel_id=1, source_target_pairs={{0,1},{1,2},{2,3},{3,4},{4,5},{5,6},{6,7},{7,8},{8,9},{9,10},{10,1... | collective-permute-start | bytes 10376 | tf_op jit(solution)/shard_map/ppermute | solution.py:15
  113.6 14.0 %collective-permute-start.10 = (bf16[96,18,1]{2,0,1:T(8,128)(2,1)}, bf16[96,18,1]{2,0,1:T(8,128)(2,1)}, u32[]{:S(2)}, u32[]{:S(2)}) collective-permute-start(bf16[96,18,1]{2,0,1:T(8,128)(2,1)} %get-tuple-element.20), channel_id=1, source_target_pairs={{1,0},{2,1},{3,2},{4,3},{5,4},{6,5},{7,6},{8,7},{9,8},{10,9},{11,1... | collective-permute-start | bytes 10376 | tf_op jit(solution)/shard_map/ppermute | solution.py:17
  119.0 25.2 %all-to-all-start.1 = ((f32[16,96,96]{2,1,0:T(8,128)}), f32[16,96,96]{2,1,0:T(8,128)S(1)}, u32[]{:S(2)}, u32[]{:S(2)}) async-start(f32[16,96,96]{2,1,0:T(8,128)} %bitcast.103), calls=%async_computation.1 | async-start | bytes 1572864 | tf_op jit(solution)/shard_map/all_to_all | solution.py:31
  131.1 3.0 %copy-start.5 = (bf16[9,96,96]{2,1,0:T(8,128)(2,1)S(1)}, bf16[9,96,96]{2,1,0:T(8,128)(2,1)}, u32[]{:S(2)}) copy-start(bf16[9,96,96]{2,1,0:T(8,128)(2,1)} %copy.113) | copy-start | bytes 497668
  131.2 2.9 %copy-start.7 = (bf16[864,16,256]{2,0,1:T(8,128)(2,1)}, bf16[864,16,256]{2,0,1:T(8,128)(2,1)S(1)}, u32[]{:S(2)}) copy-start(bf16[864,16,256]{2,0,1:T(8,128)(2,1)S(1)} %slice_dynamic-update-slice_fusion) | copy-start | bytes 21233668
  144.2 22.8 %all-to-all-start = ((f32[16,18,6,96]{3,2,1,0:T(8,128)}), f32[16,18,6,96]{3,2,1,0:T(8,128)S(1)}, u32[]{:S(2)}, u32[]{:S(2)}) async-start(f32[16,18,6,96]{3,2,1,0:T(8,128)} %copy.117), calls=%async_computation | async-start | bytes 2359296 | tf_op jit(solution)/shard_map/all_to_all | solution.py:31
where the time goes:
time: 260 us; the launch traced here: 259 us
  blocking collectives  86.6 us (33%)
  starting transfers between devices  51.3 us (20%)
  local copies, waits for them, and re-layouts  37.8 us (15%)
  matrix products  37.7 us (15%)
  waiting for transfers between devices  37 us (14%)
  other arithmetic  7.23 us (3%)
    all_to_all x1, blocking collectives, from_everyone(): lax.all_to_all(jnp.broadcast_to(value[None], (devices, *value.shape)), ax...  44.9 us
    unnamed x42, local copies, waits for them, and re-layouts  30.1 us
    ppermute x6, starting transfers between devices, padded_2(): lax.ppermute(tail, axis, [(i, (i + 1) % count) for i in range(ends)])  26.9 us
    all_gather x1, blocking collectives, shards(): lax.all_gather(rowed[2], 'col', axis=1, tiled=True)  21.9 us
    all_gather x1, blocking collectives, in_one_piece_2(): result = lax.all_gather(both, axis, axis=dim, tiled=True)  19.8 us
    all_to_all x2, waiting for transfers between devices, summed_on_arrival(): lax.all_to_all(in_blocks(value, dim, devices), axis, 0, 0, tiled=True)  17 us
    ppermute x6, waiting for transfers between devices, padded_2(): lax.ppermute(head, axis, [((i + 1) % count, i) for i in range(ends)])  16.7 us
    all_to_all x2, starting transfers between devices, summed_on_arrival(): lax.all_to_all(in_blocks(value, dim, devices), axis, 0, 0, tiled=True)  14.3 us
  transfers between devices with their start and end apart: 14, of which 6 were waited for; matrix products, arithmetic and copies ran while one was open for 15% of the time, Pallas kernels for 0%

commit v1 on v0

--- a/solution.py
+++ b/solution.py
@@ -1,7 +1,207 @@
+import functools
+
 import jax
 import jax.numpy as jnp
 from jax import lax
+from jax.experimental import pallas as pl
+from jax.experimental.pallas import tpu as pltpu
 from jax.sharding import PartitionSpec as P
+
+MESH = pl.DeviceIdType.MESH
+ROWS = 3072
+HALF = 1536
+COLOUR = 768
+BIG = 192
+SMALL = 48
+
+
+def place():
+    row, col = lax.axis_index("row"), lax.axis_index("col")
+    return dict(
+        x=(row % 2) * 2 + col // 8, y=(col // 2) % 4, z=row // 2, core=col % 2
+    )
+
+
+def device(at, **moved):
+    p = dict(at, **moved)
+    return (p["z"] * 2 + p["x"] // 2, ((p["x"] % 2) * 4 + p["y"]) * 2 + p["core"])
+
+
+def peers(at):
+    yield device(at, core=1 - at["core"])
+    for axis, n in (("x", 4), ("y", 4), ("z", 8)):
+        for step in range(1, n):
+            yield device(at, **{axis: (at[axis] + step) % n})
+
+
+def reduce_kernel(v, gin, gout, gproj, r, w, in0, in1, in2, out3, in3, sums3, sent, got):
+    at = place()
+    barrier = pltpu.get_barrier_semaphore()
+    for peer in peers(at):
+        pl.semaphore_signal(barrier, inc=1, device_id=peer, device_id_type=MESH)
+    pl.semaphore_wait(barrier, 14)
+
+    number = iter(range(100))
+
+    def copy(src, dst, peer):
+        k = next(number)
+        c = pltpu.make_async_remote_copy(
+            src_ref=src,
+            dst_ref=dst,
+            send_sem=sent.at[k],
+            recv_sem=got.at[k],
+            device_id=peer,
+            device_id_type=MESH,
+        )
+        c.start()
+        return c
+
+    def al(x, m):
+        return pl.multiple_of(x, m)
+
+    started = []
+    core = at["core"]
+    c = copy(v.at[pl.ds(al((1 - core) * HALF, 8), HALF)], in0, device(at, core=1 - core))
+    started.append(c)
+    c.wait_recv()
+    mine = al(core * HALF, 8)
+    w[...] = v[pl.ds(mine, HALF)] + in0[...]
+
+    orders = (("x", "y"), ("y", "x"))
+    starts = []
+    waits = []
+    for colour, (first, second) in enumerate(orders):
+        base = colour * COLOUR
+        row = []
+        for step in range(1, 4):
+            q = (at[first] + step) % 4
+            row.append(
+                copy(
+                    w.at[pl.ds(al(base + q * BIG, 8), BIG)],
+                    in1.at[colour, step - 1],
+                    device(at, **{first: q}),
+                )
+            )
+        waits.append(row)
+    for colour, (first, second) in enumerate(orders):
+        for c in waits[colour]:
+            c.wait_recv()
+        start = al(colour * COLOUR + at[first] * BIG, 8)
+        w[pl.ds(start, BIG)] = (
+            w[pl.ds(start, BIG)] + in1[colour, 0] + in1[colour, 1] + in1[colour, 2]
+        )
+        starts.append(start)
+        started += waits[colour]
+    waits = []
+    for colour, (first, second) in enumerate(orders):
+        row = []
+        for step in range(1, 4):
+            q = (at[second] + step) % 4
+            row.append(
+                copy(
+                    w.at[pl.ds(al(starts[colour] + q * SMALL, 8), SMALL)],
+                    in2.at[colour, step - 1],
+                    device(at, **{second: q}),
+                )
+            )
+        waits.append(row)
+    smalls = []
+    for colour, (first, second) in enumerate(orders):
+        for c in waits[colour]:
+            c.wait_recv()
+        start = al(starts[colour] + at[second] * SMALL, 8)
+        total = w[pl.ds(start, SMALL)] + in2[colour, 0] + in2[colour, 1] + in2[colour, 2]
+        out3[pl.ds(colour * 12, 12)] = total.reshape(12, 4, 128)
+        smalls.append(start)
+        started += waits[colour]
+    z = at["z"]
+    row = []
+    for step in range(1, 8):
+        q = (z + step) % 8
+        row.append(copy(out3.at[pl.ds(q * 3, 3)], in3.at[step - 1], device(at, z=q)))
+    for c in row:
+        c.wait_recv()
+    started += row
+    total = out3[pl.ds(z * 3, 3)]
+    for k in range(7):
+        total = total + in3[k]
+    sums3[pl.ds(z * 3, 3)] = total
+    row = []
+    for step in range(1, 8):
+        q = (z + step) % 8
+        row.append(
+            copy(sums3.at[pl.ds(z * 3, 3)], sums3.at[pl.ds(z * 3, 3)], device(at, z=q))
+        )
+    for c in row:
+        c.wait_recv()
+    started += row
+    waits = []
+    for colour, (first, second) in enumerate(orders):
+        rows = pl.ds(al(mine + smalls[colour], 8), SMALL)
+        r[rows] = sums3[pl.ds(colour * 12, 12)].reshape(SMALL, 128)
+        for step in range(1, 4):
+            q = (at[second] + step) % 4
+            waits.append(copy(r.at[rows], r.at[rows], device(at, **{second: q})))
+    for c in waits:
+        c.wait_recv()
+    started += waits
+    waits = []
+    other = device(at, core=1 - core)
+    last = []
+    for colour, (first, second) in enumerate(orders):
+        rows = pl.ds(al(mine + starts[colour], 8), BIG)
+        for step in range(1, 4):
+            q = (at[first] + step) % 4
+            waits.append(copy(r.at[rows], r.at[rows], device(at, **{first: q})))
+        last.append(copy(r.at[rows], r.at[rows], other))
+    k = 0
+    for colour, (first, second) in enumerate(orders):
+        for step in range(1, 4):
+            q = (at[first] - step + 4) % 4
+            rows = pl.ds(al(mine + colour * COLOUR + q * BIG, 8), BIG)
+            waits[k].wait_recv()
+            last.append(copy(r.at[rows], r.at[rows], other))
+            k += 1
+    for c in last:
+        c.wait_recv()
+    started += waits + last
+    for c in started:
+        c.wait_send()
+    for t in range(9):
+        gin[t] = r[t * 96 : (t + 1) * 96, :96]
+        gout[t] = r[864 + t * 96 : 864 + (t + 1) * 96, :96]
+    for t in range(12):
+        gproj[:, t * 128 : (t + 1) * 128] = r[1728 + t * 96 : 1728 + (t + 1) * 96]
+
+
+def all_reduce(v):
+    f32 = jnp.float32
+    vmem = pl.BlockSpec(memory_space=pltpu.VMEM)
+    return pl.pallas_call(
+        reduce_kernel,
+        out_shape=(
+            jax.ShapeDtypeStruct((9, 96, 96), f32),
+            jax.ShapeDtypeStruct((9, 96, 96), f32),
+            jax.ShapeDtypeStruct((96, 1536), f32),
+        ),
+        in_specs=[vmem],
+        out_specs=(vmem, vmem, vmem),
+        scratch_shapes=[
+            pltpu.VMEM((ROWS, 128), f32),
+            pltpu.VMEM((HALF, 128), f32),
+            pltpu.VMEM((HALF, 128), f32),
+            pltpu.VMEM((2, 3, BIG, 128), f32),
+            pltpu.VMEM((2, 3, SMALL, 128), f32),
+            pltpu.VMEM((24, 4, 128), f32),
+            pltpu.VMEM((7, 3, 4, 128), f32),
+            pltpu.VMEM((24, 4, 128), f32),
+            pltpu.SemaphoreType.DMA((48,)),
+            pltpu.SemaphoreType.DMA((48,)),
+        ],
+        compiler_params=pltpu.CompilerParams(
+            collective_id=1, has_side_effects=True, vmem_limit_bytes=40 * 2**20
+        ),
+    )(v)
 
 
 def padded_2(cells, sides, width):
@@ -19,52 +219,6 @@
             axis=dim,
         )
     return cells
-
-
-def in_blocks(value, dim, devices):
-    before, after = (value.shape[:dim], value.shape[dim + 1 :])
-    return jnp.moveaxis(value.reshape(*before, devices, -1, *after), dim, 0)
-
-
-def summed_on_arrival(value, axis, dim):
-    devices = lax.axis_size(axis)
-    parts = lax.all_to_all(in_blocks(value, dim, devices), axis, 0, 0, tiled=True)
-    return jnp.sum(parts, axis=0)
-
-
-def in_one_piece(arrays, axis, dim, along):
-    ends, at = ([], 0)
-    for a in arrays[:-1]:
-        at += a.shape[along]
-        ends.append(at)
-    both = jnp.concatenate(arrays, axis=along)
-    return tuple(jnp.split(summed_on_arrival(both, axis, dim), ends, axis=along))
-
-
-def from_everyone(value, axis):
-    devices = lax.axis_size(axis)
-    return lax.all_to_all(
-        jnp.broadcast_to(value[None], (devices, *value.shape)), axis, 0, 0, tiled=True
-    )
-
-
-def of_everyone(value, axis):
-    return from_everyone(value, axis).sum(axis=0)
-
-
-def in_one(arrays, axis):
-    ends = [0]
-    for a in arrays:
-        ends.append(ends[-1] + a.size)
-    so_far = of_everyone(jnp.concatenate([a.ravel() for a in arrays]), axis)
-    return tuple((so_far[b:e].reshape(a.shape) for a, b, e in zip(arrays, ends, ends[1:])))
-
-
-def in_one_piece_2(arrays, axis, dim, along):
-    widths = [a.shape[along] for a in arrays]
-    both = jnp.concatenate(arrays, axis=along)
-    result = lax.all_gather(both, axis, axis=dim, tiled=True)
-    return tuple(jnp.split(result, [sum(widths[:k]) for k in range(1, len(widths))], axis=along))
 
 
 def gelu_grad(value):
@@ -123,16 +277,15 @@
     grad_in = jnp.einsum("khw,ohw->ko", x_taps, dpre, preferred_element_type=jnp.float32).reshape(
         9, chans, chans
     )
-    owned = (
-        *in_one_piece((grad_in, grad_out), "col", 1, 0),
-        summed_on_arrival(grad_proj, "col", 1),
-    )
-    rowed = in_one((owned[0], owned[1], owned[2]), "row")
-    result = (
-        *in_one_piece_2((rowed[0], rowed[1]), "col", 1, 0),
-        lax.all_gather(rowed[2], "col", axis=1, tiled=True),
-    )
-    return (result[0], result[1], result[2])
+    flat = jnp.concatenate(
+        [
+            jnp.pad(grad_in.reshape(864, 96), ((0, 0), (0, 32))),
+            jnp.pad(grad_out.reshape(864, 96), ((0, 0), (0, 32))),
+            grad_proj.reshape(96, 12, 128).transpose(1, 0, 2).reshape(1152, 128),
+            jnp.zeros((192, 128), jnp.float32),
+        ]
+    )
+    return all_reduce(flat)
 
 
 def solution(mesh):

time: 260 us -> 191 us (0.73)
  blocking collectives: 86.6 us -> 0 us
  Pallas kernels: 0 us -> 49.5 us
  starting transfers between devices: 51.3 us -> 37.2 us
  waiting for transfers between devices: 37 us -> 24.6 us
  local copies, waits for them, and re-layouts: 37.8 us -> 33.6 us
    pallas_call x0 -> x1, Pallas kernels: none -> 49.5 us  [all_reduce(): pl.pallas_call(reduce_kernel, out_shape=(jax.ShapeDtypeStruct((9, 96, 96)...]
    all_to_all x1 -> x0, blocking collectives: 44.9 us -> none  [from_everyone(): lax.all_to_all(jnp.broadcast_to(value[None], (devices, *value.shape)), ax...]
    all_gather x2 -> x0, blocking collectives: 41.7 us -> none  [the longest x1 21.9 us: shards(): lax.all_gather(rowed[2], 'col', axis=1, tiled=True)]
    all_to_all x2 -> x0, waiting for transfers between devices: 17 us -> none  [summed_on_arrival(): lax.all_to_all(in_blocks(value, dim, devices), axis, 0, 0, tiled=True)]
    all_to_all x2 -> x0, starting transfers between devices: 14.3 us -> none  [summed_on_arrival(): lax.all_to_all(in_blocks(value, dim, devices), axis, 0, 0, tiled=True)]
    ppermute x6, waiting for transfers between devices: 16.7 us -> 21 us  [padded_2(): lax.ppermute(head, axis, [((i + 1) % count, i) for i in range(ends)])]
    unnamed x42 -> x44, local copies, waits for them, and re-layouts: 30.1 us -> 29.7 us
  transfers between devices with their start and end apart: 14 -> 12, of which waited for: 6 -> 7; matrix products, arithmetic and copies ran while one was open for 15% -> 12% of each run, Pallas kernels for 0% -> 0%
where the time goes in v1:
time: 191 us; the launch traced here: 190 us
  Pallas kernels  49.5 us (26%)
  matrix products  38.6 us (20%)
  starting transfers between devices  37.2 us (19%)
  local copies, waits for them, and re-layouts  33.6 us (18%)
  waiting for transfers between devices  24.6 us (13%)
  other arithmetic  5.48 us (3%)
    pallas_call x1, Pallas kernels, all_reduce(): pl.pallas_call(reduce_kernel, out_shape=(jax.ShapeDtypeStruct((9, 96, 96)...  49.5 us
    unnamed x44, local copies, waits for them, and re-layouts  29.7 us
    ppermute x6, starting transfers between devices, padded_2(): lax.ppermute(tail, axis, [(i, (i + 1) % count) for i in range(ends)])  26.9 us
    ppermute x6, waiting for transfers between devices, padded_2(): lax.ppermute(head, axis, [((i + 1) % count, i) for i in range(ends)])  21 us
    ppermute x6, starting transfers between devices, padded_2(): lax.ppermute(head, axis, [((i + 1) % count, i) for i in range(ends)])  10.2 us
    dot_general x1, matrix products, shards(): jnp.einsum('ce,chw->ehw', projector, student, preferred_element_type=jnp....  9.21 us
    dot_general x1, matrix products, shards(): jnp.einsum('khw,ohw->ko', x_taps, dpre, preferred_element_type=jnp.float32)  8.82 us
    dot_general x1, matrix products, shards(): jnp.einsum('ce,ehw->chw', projector, dpred, preferred_element_type=jnp.fl...  8.61 us
  transfers between devices with their start and end apart: 12, of which 7 were waited for; matrix products, arithmetic and copies ran while one was open for 12% of the time, Pallas kernels for 0%

profile of v1, /device:TPU:1, one launch (start us, length us, event | category | flops | bytes accessed | tf_op | source)
XLA Modules:
  0.0 190.2 jit_solution(9799602817711337336)
XLA Ops:
  0.7 1.5 copy.23
  2.1 5.5 %collective-permute-start = (bf16[96,1,256]{2,0,1:T(8,128)(2,1)S(1)}, bf16[96,1,256]{2,0,1:T(8,128)(2,1)S(1)}, u32[]{:S(2)}, u32[]{:S(2)}) collective-permute-start(bf16[96,1,256]{2,0,1:T(8,128)(2,1)S(1)} %get-tuple-element.18), channel_id=1, source_target_pairs={{0,16},{16,32},{32,48},{48,64},{64,80},{80,96},{96,112},{112,128},... | collective-permute-start | bytes 147464 | tf_op jit(solution)/shard_map/ppermute | solution.py:215
  7.6 1.3 collective-permute-start.1
  9.2 4.8 %collective-permute-done.1 = bf16[96,1,256]{2,0,1:T(8,128)(2,1)S(1)} collective-permute-done((bf16[96,1,256]{2,0,1:T(8,128)(2,1)S(1)}, bf16[96,1,256]{2,0,1:T(8,128)(2,1)S(1)}, u32[]{:S(2)}, u32[]{:S(2)}) %collective-permute-start.1) | collective-permute-done | bytes 49184 | tf_op jit(solution)/shard_map/ppermute | solution.py:217
  14.2 5.2 %collective-permute-start.2 = (bf16[96,18,1]{2,0,1:T(8,128)(2,1)S(1)}, bf16[96,18,1]{2,0,1:T(8,128)(2,1)S(1)}, u32[]{:S(2)}, u32[]{:S(2)}) collective-permute-start(bf16[96,18,1]{2,0,1:T(8,128)(2,1)S(1)} %get-tuple-element.12), channel_id=1, source_target_pairs={{0,1},{1,2},{2,3},{3,4},{4,5},{5,6},{6,7},{7,8},{8,9},{9,10},{10,1... | collective-permute-start | bytes 10376 | tf_op jit(solution)/shard_map/ppermute | solution.py:215
  19.4 1.9 %collective-permute-start.3 = (bf16[96,18,1]{2,0,1:T(8,128)(2,1)S(1)}, bf16[96,18,1]{2,0,1:T(8,128)(2,1)S(1)}, u32[]{:S(2)}, u32[]{:S(2)}) collective-permute-start(bf16[96,18,1]{2,0,1:T(8,128)(2,1)S(1)} %get-tuple-element.11), channel_id=1, source_target_pairs={{1,0},{2,1},{3,2},{4,3},{5,4},{6,5},{7,6},{8,7},{9,8},{10,9},{11,1... | collective-permute-start | bytes 10376 | tf_op jit(solution)/shard_map/ppermute | solution.py:217
  21.3 3.3 %collective-permute-done.2 = bf16[96,18,1]{2,0,1:T(8,128)(2,1)S(1)} collective-permute-done((bf16[96,18,1]{2,0,1:T(8,128)(2,1)S(1)}, bf16[96,18,1]{2,0,1:T(8,128)(2,1)S(1)}, u32[]{:S(2)}, u32[]{:S(2)}) %collective-permute-start.2) | collective-permute-done | bytes 3488 | tf_op jit(solution)/shard_map/ppermute | solution.py:215
  25.0 4.0 %collective-permute-done.3 = bf16[96,18,1]{2,0,1:T(8,128)(2,1)S(1)} collective-permute-done((bf16[96,18,1]{2,0,1:T(8,128)(2,1)S(1)}, bf16[96,18,1]{2,0,1:T(8,128)(2,1)S(1)}, u32[]{:S(2)}, u32[]{:S(2)}) %collective-permute-start.3) | collective-permute-done | bytes 3488 | tf_op jit(solution)/shard_map/ppermute | solution.py:217
  29.0 0.4 fusion.33
  29.4 0.4 fusion.35
  30.1 0.4 fusion.31
  30.5 0.4 fusion.44
  31.0 0.4 fusion.42
  31.4 0.4 copy-done.9
  31.8 5.5 %fusion.4 = (bf16[96,16,256]{2,0,1:T(8,128)(2,1)S(1)}, f32[16,256,96]{1,2,0:T(8,128)}) fusion(bf16[864,16,256]{2,0,1:T(8,128)(2,1)S(1)} %fusion.42, bf16[864,96,1]{1,0,2:T(8,128)(2,1)S(1)} %bitcast.108), kind=kOutput, calls=%fused_computation.14 | convolution fusion | flops 705036288 | bytes 9603072 | tf_op jit(solution)/shard_map/ko,khw->ohw/dot_general | solution.py:252
  37.4 4.4 %collective-permute-start.4 = (bf16[96,1,256]{2,0,1:T(8,128)(2,1)S(1)}, bf16[96,1,256]{2,0,1:T(8,128)(2,1)S(1)}, u32[]{:S(2)}, u32[]{:S(2)}) collective-permute-start(bf16[96,1,256]{2,0,1:T(8,128)(2,1)S(1)} %get-tuple-element.15), channel_id=1, source_target_pairs={{0,16},{16,32},{32,48},{48,64},{64,80},{80,96},{96,112},{112,128},... | collective-permute-start | bytes 147464 | tf_op jit(solution)/shard_map/ppermute | solution.py:215
  41.8 1.4 collective-permute-start.5
  43.3 5.0 %collective-permute-done.5 = bf16[96,1,256]{2,0,1:T(8,128)(2,1)S(1)} collective-permute-done((bf16[96,1,256]{2,0,1:T(8,128)(2,1)S(1)}, bf16[96,1,256]{2,0,1:T(8,128)(2,1)S(1)}, u32[]{:S(2)}, u32[]{:S(2)}) %collective-permute-start.5) | collective-permute-done | bytes 49184 | tf_op jit(solution)/shard_map/ppermute | solution.py:217
  48.4 1.0 fusion.54
  49.4 1.9 %collective-permute-start.7 = (bf16[96,18,1]{2,0,1:T(8,128)(2,1)}, bf16[96,18,1]{2,0,1:T(8,128)(2,1)S(1)}, u32[]{:S(2)}, u32[]{:S(2)}) collective-permute-start(bf16[96,18,1]{2,0,1:T(8,128)(2,1)} %get-tuple-element.9), channel_id=1, source_target_pairs={{1,0},{2,1},{3,2},{4,3},{5,4},{6,5},{7,6},{8,7},{9,8},{10,9},{11,1... | collective-permute-start | bytes 10376 | tf_op jit(solution)/shard_map/ppermute | solution.py:217
  51.3 3.8 %collective-permute-start.6 = (bf16[96,18,1]{2,0,1:T(8,128)(2,1)S(1)}, bf16[96,18,1]{2,0,1:T(8,128)(2,1)S(1)}, u32[]{:S(2)}, u32[]{:S(2)}) collective-permute-start(bf16[96,18,1]{2,0,1:T(8,128)(2,1)S(1)} %get-tuple-element.10), channel_id=1, source_target_pairs={{0,1},{1,2},{2,3},{3,4},{4,5},{5,6},{6,7},{7,8},{8,9},{9,10},{10,1... | collective-permute-start | bytes 10376 | tf_op jit(solution)/shard_map/ppermute | solution.py:215
  55.1 0.8 copy.34
  56.0 16.9 %copy.32 = bf16[1536,16,256]{0,2,1:T(8,128)(2,1)} copy(bf16[1536,16,256]{2,1,0:T(8,128)(2,1)} %param.6) | data formatting | bytes 25165824 | tf_op args[1]
  73.0 1.0 pad_maximum_fusion
  74.1 0.4 slice_dynamic-update-slice_fusion.10
  75.5 2.9 %copy-done.2 = bf16[864,16,256]{2,0,1:T(8,128)(2,1)} copy-done((bf16[864,16,256]{2,0,1:T(8,128)(2,1)}, bf16[864,16,256]{2,0,1:T(8,128)(2,1)S(1)}, u32[]{:S(2)}) %copy-start.2) | copy-done | bytes 7077912
  78.4 1.5 fusion.13
  79.9 9.2 %fusion.1 = bf16[1536,16,256]{0,2,1:T(8,128)(2,1)} fusion(bf16[1536,16,256]{0,2,1:T(8,128)(2,1)} %copy.32, bf16[96,16,256]{2,0,1:T(8,128)(2,1)S(1)} %fusion.13, bf16[96,1536]{1,0:T(8,128)(2,1)S(1)} %copy-done), kind=kOutput, calls=%fused_computation.2 | convolution fusion | flops 1233125376 | bytes 26247168 | tf_op jit(solution)/shard_map/ce,chw->ehw/dot_general | solution.py:258
  89.2 8.6 %fusion.29 = bf16[96,16,256]{2,0,1:T(8,128)(2,1)S(1)} fusion(bf16[1536,16,256]{0,2,1:T(8,128)(2,1)} %fusion.1, bf16[96,1536]{1,0:T(8,128)(2,1)S(1)} %copy-done), kind=kOutput, calls=%fused_computation.60 | convolution fusion | flops 1208352768 | bytes 13664256 | tf_op jit(solution)/shard_map/ce,ehw->chw/dot_general | solution.py:262
  97.8 4.7 %collective-permute-start.8 = (bf16[96,1,256]{2,0,1:T(8,128)(2,1)S(1)}, bf16[96,1,256]{2,0,1:T(8,128)(2,1)S(1)}, u32[]{:S(2)}, u32[]{:S(2)}) collective-permute-start(bf16[96,1,256]{2,0,1:T(8,128)(2,1)S(1)} %get-tuple-element.13), channel_id=1, source_target_pairs={{0,16},{16,32},{32,48},{48,64},{64,80},{80,96},{96,112},{112,128},... | collective-permute-start | bytes 147464 | tf_op jit(solution)/shard_map/ppermute | solution.py:215
  102.5 1.6 collective-permute-start.9
  104.0 2.1 %convolution_bitcast_fusion = f32[96,1536]{1,0:T(8,128)S(1)} fusion(bf16[96,16,256]{2,0,1:T(8,128)(2,1)S(1)} %fusion.13, bf16[1536,16,256]{0,2,1:T(8,128)(2,1)S(1)} %copy-done.1), kind=kOutput, calls=%fused_computation.3 | convolution fusion | flops 1207959552 | bytes 13959168 | tf_op jit(solution)/shard_map/chw,ehw->ce/dot_general | solution.py:261
  106.2 3.0 %collective-permute-done.9 = bf16[96,1,256]{2,0,1:T(8,128)(2,1)S(1)} collective-permute-done((bf16[96,1,256]{2,0,1:T(8,128)(2,1)S(1)}, bf16[96,1,256]{2,0,1:T(8,128)(2,1)S(1)}, u32[]{:S(2)}, u32[]{:S(2)}) %collective-permute-start.9) | collective-permute-done | bytes 49184 | tf_op jit(solution)/shard_map/ppermute | solution.py:217
  109.3 1.1 fusion.53
  110.4 3.4 %collective-permute-start.11 = (bf16[96,18,1]{2,0,1:T(8,128)(2,1)}, bf16[96,18,1]{2,0,1:T(8,128)(2,1)S(1)}, u32[]{:S(2)}, u32[]{:S(2)}) collective-permute-start(bf16[96,18,1]{2,0,1:T(8,128)(2,1)} %get-tuple-element.5), channel_id=1, source_target_pairs={{0,1},{1,2},{2,3},{3,4},{4,5},{5,6},{6,7},{7,8},{8,9},{9,10},{10,1... | collective-permute-start | bytes 10376 | tf_op jit(solution)/shard_map/ppermute | solution.py:215
  113.8 2.1 %collective-permute-start.10 = (bf16[96,18,1]{2,0,1:T(8,128)(2,1)}, bf16[96,18,1]{2,0,1:T(8,128)(2,1)S(1)}, u32[]{:S(2)}, u32[]{:S(2)}) collective-permute-start(bf16[96,18,1]{2,0,1:T(8,128)(2,1)} %get-tuple-element.6), channel_id=1, source_target_pairs={{1,0},{2,1},{3,2},{4,3},{5,4},{6,5},{7,6},{8,7},{9,8},{10,9},{11,1... | collective-permute-start | bytes 10376 | tf_op jit(solution)/shard_map/ppermute | solution.py:217
  115.9 2.7 %convolution_bitcast_fusion.1 = f32[864,96]{1,0:T(8,128)} fusion(bf16[864,16,256]{2,0,1:T(8,128)(2,1)S(1)} %bitcast.102, bf16[96,16,256]{2,0,1:T(8,128)(2,1)S(1)} %fusion.29), kind=kOutput, calls=%fused_computation.61 | convolution fusion | flops 679477248 | bytes 8196096 | tf_op jit(solution)/shard_map/khw,ohw->ko/dot_general | solution.py:274
  119.3 4.3 %collective-permute-done.10 = bf16[96,18,1]{2,0,1:T(8,128)(2,1)S(1)} collective-permute-done((bf16[96,18,1]{2,0,1:T(8,128)(2,1)}, bf16[96,18,1]{2,0,1:T(8,128)(2,1)S(1)}, u32[]{:S(2)}, u32[]{:S(2)}) %collective-permute-start.10) | collective-permute-done | bytes 3488 | tf_op jit(solution)/shard_map/ppermute | solution.py:217
  123.6 1.0 maximum_maximum_fusion.1
  125.1 0.4 slice_dynamic-update-slice_fusion.3
  125.6 0.4 slice_dynamic-update-slice_fusion.1
  126.1 2.9 %copy-done.8 = bf16[864,16,256]{2,0,1:T(8,128)(2,1)} copy-done((bf16[864,16,256]{2,0,1:T(8,128)(2,1)}, bf16[864,16,256]{2,0,1:T(8,128)(2,1)S(1)}, u32[]{:S(2)}) %copy-start.8) | copy-done | bytes 7077912
  129.0 8.8 %convolution_bitcast_fusion.2 = f32[864,96]{1,0:T(8,128)S(1)} fusion(bf16[864,16,256]{2,0,1:T(8,128)(2,1)} %copy-done.7, f32[16,256,96]{1,2,0:T(8,128)} %get-tuple-element.20, bf16[864,16,256]{2,0,1:T(8,128)(2,1)} %copy-done.8, bf16[864,96,1]{1,0,2:T(8,128)(2,1)S(1)} %bitcast.107), kind=kOutput, calls=%fused_computation.62 | convolution fusion | flops 1362886656 | bytes 16226304 | tf_op jit(solution)/shard_map/khw,ohw->ko/dot_general | solution.py:277
  137.8 0.5 fusion.12.v
  138.3 49.5 %shard_map.76 = (f32[9,96,96]{2,1,0:T(8,128)S(1)}, f32[9,96,96]{2,1,0:T(8,128)S(1)}, f32[96,1536]{1,0:T(8,128)S(1)}) custom-call(f32[3072,128]{1,0:T(8,128)S(1)} %fusion.12.v), custom_call_target="tpu_custom_call" | custom-call | tf_op jit(solution)/shard_map/pallas_call | solution.py:180
  187.8 0.8 copy.81
  188.6 0.8 copy.82
  189.4 0.8 copy.83
  (60 shorter events, 4.0 us)
Async XLA Ops:
  0.6 79.3 %copy-start = (bf16[96,1536]{1,0:T(8,128)(2,1)S(1)}, bf16[96,1536]{1,0:T(8,128)(2,1)}, u32[]{:S(2)}) copy-start(bf16[96,1536]{1,0:T(8,128)(2,1)} %param.9) | copy-start | bytes 884740
  0.6 8.3 %copy-start.3 = (bf16[96,16,256]{2,1,0:T(8,128)(2,1)S(1)}, bf16[96,16,256]{2,1,0:T(8,128)(2,1)}, u32[]{:S(2)}) copy-start(bf16[96,16,256]{2,1,0:T(8,128)(2,1)} %param.5) | copy-start | bytes 2359300
  2.1 6.8 %collective-permute-start = (bf16[96,1,256]{2,0,1:T(8,128)(2,1)S(1)}, bf16[96,1,256]{2,0,1:T(8,128)(2,1)S(1)}, u32[]{:S(2)}, u32[]{:S(2)}) collective-permute-start(bf16[96,1,256]{2,0,1:T(8,128)(2,1)S(1)} %get-tuple-element.18), channel_id=1, source_target_pairs={{0,16},{16,32},{32,48},{48,64},{64,80},{80,96},{96,112},{112,128},... | collective-permute-start | bytes 147464 | tf_op jit(solution)/shard_map/ppermute | solution.py:215
  7.6 6.3 %collective-permute-start.1 = (bf16[96,1,256]{2,0,1:T(8,128)(2,1)S(1)}, bf16[96,1,256]{2,0,1:T(8,128)(2,1)S(1)}, u32[]{:S(2)}, u32[]{:S(2)}) collective-permute-start(bf16[96,1,256]{2,0,1:T(8,128)(2,1)S(1)} %get-tuple-element.17), channel_id=1, source_target_pairs={{16,0},{32,16},{48,32},{64,48},{80,64},{96,80},{112,96},{128,112},... | collective-permute-start | bytes 147464 | tf_op jit(solution)/shard_map/ppermute | solution.py:217
  14.2 10.4 %collective-permute-start.2 = (bf16[96,18,1]{2,0,1:T(8,128)(2,1)S(1)}, bf16[96,18,1]{2,0,1:T(8,128)(2,1)S(1)}, u32[]{:S(2)}, u32[]{:S(2)}) collective-permute-start(bf16[96,18,1]{2,0,1:T(8,128)(2,1)S(1)} %get-tuple-element.12), channel_id=1, source_target_pairs={{0,1},{1,2},{2,3},{3,4},{4,5},{5,6},{6,7},{7,8},{8,9},{9,10},{10,1... | collective-permute-start | bytes 10376 | tf_op jit(solution)/shard_map/ppermute | solution.py:215
  19.4 9.6 %collective-permute-start.3 = (bf16[96,18,1]{2,0,1:T(8,128)(2,1)S(1)}, bf16[96,18,1]{2,0,1:T(8,128)(2,1)S(1)}, u32[]{:S(2)}, u32[]{:S(2)}) collective-permute-start(bf16[96,18,1]{2,0,1:T(8,128)(2,1)S(1)} %get-tuple-element.11), channel_id=1, source_target_pairs={{1,0},{2,1},{3,2},{4,3},{5,4},{6,5},{7,6},{8,7},{9,8},{10,9},{11,1... | collective-permute-start | bytes 10376 | tf_op jit(solution)/shard_map/ppermute | solution.py:217
  30.9 0.9 copy-start.9
  31.4 6.0 %copy-start.7 = (bf16[864,16,256]{2,0,1:T(8,128)(2,1)}, bf16[864,16,256]{2,0,1:T(8,128)(2,1)S(1)}, u32[]{:S(2)}) copy-start(bf16[864,16,256]{2,0,1:T(8,128)(2,1)S(1)} %fusion.42) | copy-start | bytes 21233668
  37.4 5.8 %collective-permute-start.4 = (bf16[96,1,256]{2,0,1:T(8,128)(2,1)S(1)}, bf16[96,1,256]{2,0,1:T(8,128)(2,1)S(1)}, u32[]{:S(2)}, u32[]{:S(2)}) collective-permute-start(bf16[96,1,256]{2,0,1:T(8,128)(2,1)S(1)} %get-tuple-element.15), channel_id=1, source_target_pairs={{0,16},{16,32},{32,48},{48,64},{64,80},{80,96},{96,112},{112,128},... | collective-permute-start | bytes 147464 | tf_op jit(solution)/shard_map/ppermute | solution.py:215
  41.8 13.3 %copy-start.4 = (bf16[9,96,96]{2,1,0:T(8,128)(2,1)S(1)}, bf16[9,96,96]{2,1,0:T(8,128)(2,1)}, u32[]{:S(2)}) copy-start(bf16[9,96,96]{2,1,0:T(8,128)(2,1)} %param.8) | copy-start | bytes 497668
  41.8 6.5 %collective-permute-start.5 = (bf16[96,1,256]{2,0,1:T(8,128)(2,1)S(1)}, bf16[96,1,256]{2,0,1:T(8,128)(2,1)S(1)}, u32[]{:S(2)}, u32[]{:S(2)}) collective-permute-start(bf16[96,1,256]{2,0,1:T(8,128)(2,1)S(1)} %get-tuple-element.16), channel_id=1, source_target_pairs={{16,0},{32,16},{48,32},{64,48},{80,64},{96,80},{112,96},{128,112},... | collective-permute-start | bytes 147464 | tf_op jit(solution)/shard_map/ppermute | solution.py:217
  49.4 23.6 %collective-permute-start.7 = (bf16[96,18,1]{2,0,1:T(8,128)(2,1)}, bf16[96,18,1]{2,0,1:T(8,128)(2,1)S(1)}, u32[]{:S(2)}, u32[]{:S(2)}) collective-permute-start(bf16[96,18,1]{2,0,1:T(8,128)(2,1)} %get-tuple-element.9), channel_id=1, source_target_pairs={{1,0},{2,1},{3,2},{4,3},{5,4},{6,5},{7,6},{8,7},{9,8},{10,9},{11,1... | collective-permute-start | bytes 10376 | tf_op jit(solution)/shard_map/ppermute | solution.py:217
  51.3 21.7 %collective-permute-start.6 = (bf16[96,18,1]{2,0,1:T(8,128)(2,1)S(1)}, bf16[96,18,1]{2,0,1:T(8,128)(2,1)S(1)}, u32[]{:S(2)}, u32[]{:S(2)}) collective-permute-start(bf16[96,18,1]{2,0,1:T(8,128)(2,1)S(1)} %get-tuple-element.10), channel_id=1, source_target_pairs={{0,1},{1,2},{2,3},{3,4},{4,5},{5,6},{6,7},{7,8},{8,9},{9,10},{10,1... | collective-permute-start | bytes 10376 | tf_op jit(solution)/shard_map/ppermute | solution.py:215
  75.5 2.9 %copy-start.2 = (bf16[864,16,256]{2,0,1:T(8,128)(2,1)}, bf16[864,16,256]{2,0,1:T(8,128)(2,1)S(1)}, u32[]{:S(2)}) copy-start(bf16[864,16,256]{2,0,1:T(8,128)(2,1)S(1)} %slice_dynamic-update-slice_fusion.6) | copy-start | bytes 21233668
  89.2 14.9 %copy-start.1 = (bf16[1536,16,256]{0,2,1:T(8,128)(2,1)S(1)}, bf16[1536,16,256]{0,2,1:T(8,128)(2,1)}, u32[]{:S(2)}) copy-start(bf16[1536,16,256]{0,2,1:T(8,128)(2,1)} %fusion.1) | copy-start | bytes 37748740
  97.8 8.4 %collective-permute-start.8 = (bf16[96,1,256]{2,0,1:T(8,128)(2,1)S(1)}, bf16[96,1,256]{2,0,1:T(8,128)(2,1)S(1)}, u32[]{:S(2)}, u32[]{:S(2)}) collective-permute-start(bf16[96,1,256]{2,0,1:T(8,128)(2,1)S(1)} %get-tuple-element.13), channel_id=1, source_target_pairs={{0,16},{16,32},{32,48},{48,64},{64,80},{80,96},{96,112},{112,128},... | collective-permute-start | bytes 147464 | tf_op jit(solution)/shard_map/ppermute | solution.py:215
  102.5 13.5 %slice-start = ((s8[7077888]{0:T(1024)(128)(4,1)}), s8[4194304]{0:T(1024)(128)(4,1)S(1)}, s32[]{:S(2)}) async-start(s8[7077888]{0:T(1024)(128)(4,1)} %bitcast.101), calls=%async_computation | async-start | bytes 8388608
  102.5 13.5 %slice-start.1 = ((s8[7077888]{0:T(1024)(128)(4,1)}), s8[2883584]{0:T(1024)(128)(4,1)S(1)}, s32[]{:S(2)}) async-start(s8[7077888]{0:T(1024)(128)(4,1)} %bitcast.101), calls=%async_computation.1 | async-start | bytes 5767168
  102.5 6.7 %collective-permute-start.9 = (bf16[96,1,256]{2,0,1:T(8,128)(2,1)S(1)}, bf16[96,1,256]{2,0,1:T(8,128)(2,1)S(1)}, u32[]{:S(2)}, u32[]{:S(2)}) collective-permute-start(bf16[96,1,256]{2,0,1:T(8,128)(2,1)S(1)} %get-tuple-element.14), channel_id=1, source_target_pairs={{16,0},{32,16},{48,32},{64,48},{80,64},{96,80},{112,96},{128,112},... | collective-permute-start | bytes 147464 | tf_op jit(solution)/shard_map/ppermute | solution.py:217
  110.4 8.9 %collective-permute-start.11 = (bf16[96,18,1]{2,0,1:T(8,128)(2,1)}, bf16[96,18,1]{2,0,1:T(8,128)(2,1)S(1)}, u32[]{:S(2)}, u32[]{:S(2)}) collective-permute-start(bf16[96,18,1]{2,0,1:T(8,128)(2,1)} %get-tuple-element.5), channel_id=1, source_target_pairs={{0,1},{1,2},{2,3},{3,4},{4,5},{5,6},{6,7},{7,8},{8,9},{9,10},{10,1... | collective-permute-start | bytes 10376 | tf_op jit(solution)/shard_map/ppermute | solution.py:215
  113.8 9.8 %collective-permute-start.10 = (bf16[96,18,1]{2,0,1:T(8,128)(2,1)}, bf16[96,18,1]{2,0,1:T(8,128)(2,1)S(1)}, u32[]{:S(2)}, u32[]{:S(2)}) collective-permute-start(bf16[96,18,1]{2,0,1:T(8,128)(2,1)} %get-tuple-element.6), channel_id=1, source_target_pairs={{1,0},{2,1},{3,2},{4,3},{5,4},{6,5},{7,6},{8,7},{9,8},{10,9},{11,1... | collective-permute-start | bytes 10376 | tf_op jit(solution)/shard_map/ppermute | solution.py:217
  126.0 3.0 %copy-start.6 = (bf16[9,96,96]{2,1,0:T(8,128)(2,1)S(1)}, bf16[9,96,96]{2,1,0:T(8,128)(2,1)}, u32[]{:S(2)}) copy-start(bf16[9,96,96]{2,1,0:T(8,128)(2,1)} %copy.34) | copy-start | bytes 497668
  126.1 2.9 %copy-start.8 = (bf16[864,16,256]{2,0,1:T(8,128)(2,1)}, bf16[864,16,256]{2,0,1:T(8,128)(2,1)S(1)}, u32[]{:S(2)}) copy-start(bf16[864,16,256]{2,0,1:T(8,128)(2,1)S(1)} %slice_dynamic-update-slice_fusion) | copy-start | bytes 21233668
  129.0 8.8 %copy-start.5 = (f32[864,96]{1,0:T(8,128)S(1)}, f32[864,96]{1,0:T(8,128)}, u32[]{:S(2)}) copy-start(f32[864,96]{1,0:T(8,128)} %convolution_bitcast_fusion.1) | copy-start | bytes 995332

commit v2 on v1

--- a/solution.py
+++ b/solution.py
@@ -202,90 +202,272 @@
             collective_id=1, has_side_effects=True, vmem_limit_bytes=40 * 2**20
         ),
     )(v)
-
-
-def padded_2(cells, sides, width):
-    for axis, dim in sides:
-        count = lax.axis_size(axis)
-        ends = count - 1
-        head = lax.slice_in_dim(cells, 0, width, axis=dim)
-        tail = lax.slice_in_dim(cells, cells.shape[dim] - width, cells.shape[dim], axis=dim)
-        cells = jnp.concatenate(
-            [
-                lax.ppermute(tail, axis, [(i, (i + 1) % count) for i in range(ends)]),
-                cells,
-                lax.ppermute(head, axis, [((i + 1) % count, i) for i in range(ends)]),
-            ],
-            axis=dim,
+AROUND = ((-1, 0), (1, 0), (0, -1), (0, 1), (-1, -1), (-1, 1), (1, -1), (1, 1))
+SCALE = 2.0**-20
+CHUNK = 256
+
+
+def dot(a, b):
+    return jnp.dot(a, b, preferred_element_type=jnp.float32)
+
+
+def dot_nt(a, b):
+    return lax.dot_general(a, b, (((1,), (1,)), ((), ())), preferred_element_type=jnp.float32)
+
+
+def pieces(value):
+    out = []
+    for _ in range(3):
+        out.append(value.astype(jnp.bfloat16))
+        value = value - out[-1].astype(jnp.float32)
+    return out
+
+
+def phi(value):
+    return 0.5 * (1.0 + lax.erf(value * 0.7071067811865476))
+
+
+def main_kernel(
+    feat, teach, w1, w2, wb, proj, v,
+    fv, tin, t2, xh, hh, gp, ds, lhs, gacc, taps, tile, around, local, sent, got,
+):
+    bf16, f32 = jnp.bfloat16, jnp.float32
+    rows, cols = lax.axis_size("row"), lax.axis_size("col")
+    row, col = lax.axis_index("row"), lax.axis_index("col")
+    up, down, left, right = row > 0, row < rows - 1, col > 0, col < cols - 1
+
+    def neighbour(dr, dc):
+        return ((row + dr + rows) % rows, (col + dc + cols) % cols)
+
+    feat_copy = pltpu.make_async_copy(feat, fv, local.at[0])
+    feat_copy.start()
+    t_copies = []
+    for k in range(1536 // CHUNK):
+        part = pl.ds(k * CHUNK, CHUNK)
+        t_copies.append(pltpu.make_async_copy(teach.at[part], tin.at[part], local.at[k + 1]))
+        t_copies[-1].start()
+    barrier = pltpu.get_barrier_semaphore()
+    for dr, dc in AROUND:
+        pl.semaphore_signal(barrier, inc=1, device_id=neighbour(dr, dc), device_id_type=MESH)
+
+    lane = lax.broadcasted_iota(jnp.int32, (96, 128), 1)
+    hpos = (lane * 43) >> 8
+    jpos = lane - hpos * 6
+
+    def own_tile(read):
+        def step(h, acc):
+            x = read(h).astype(f32)
+            at = (h + 2) * 6
+            hi = pltpu.roll(x[:, 128:], at + 2, 1)
+            lo = pltpu.roll(x[:, :128], at + 4, 1)
+            here = hpos == h + 2
+            acc = jnp.where(here & (jpos < 2), hi, acc)
+            return jnp.where(here & (jpos > 3), lo, acc)
+
+        return lax.fori_loop(0, 16, step, jnp.zeros((96, 128), f32))
+
+    def exchange(part, top, bottom, to_top, to_bottom):
+        copies = []
+
+        def send(k, src, dst, dr, dc):
+            c = pltpu.make_async_remote_copy(
+                src_ref=src,
+                dst_ref=dst,
+                send_sem=sent.at[part, k],
+                recv_sem=got.at[part, k],
+                device_id=neighbour(dr, dc),
+                device_id_type=MESH,
+            )
+            c.start()
+            copies.append(c)
+
+        send(8, top, to_bottom, -1, 0)
+        send(9, bottom, to_top, 1, 0)
+        for k, (dr, dc) in enumerate(AROUND):
+            send(k, tile.at[part], around.at[part, AROUND.index((-dr, -dc))], dr, dc)
+        return copies
+
+    def rim(part):
+        def get(dr, dc):
+            if (dr, dc) == (0, 0):
+                return tile[part].astype(f32)
+            return around[part, AROUND.index((dr, dc))].astype(f32)
+
+        def band(dr):
+            mid = get(dr, 0)
+            inner = jnp.where(jpos == 2, pltpu.roll(mid, 126, 1), pltpu.roll(mid, 2, 1))
+            outer = jnp.where(jpos < 2, get(dr, -1), get(dr, 1))
+            return jnp.where((jpos == 2) | (jpos == 3), inner, outer)
+
+        full = jnp.where(
+            hpos < 2,
+            pltpu.roll(band(-1), 32, 1),
+            jnp.where(hpos < 18, band(0), pltpu.roll(band(1), 96, 1)),
         )
-    return cells
-
-
-def gelu_grad(value):
-    cdf = 0.5 * (1.0 + jax.scipy.special.erf(value * 0.7071067811865476))
-    dens = jnp.exp(-0.5 * value * value) * 0.3989422804014327
-    return cdf + value * dens
-
-
-def tap_stack(padded, height, width):
-    return jnp.concatenate(
-        [padded[:, tap // 3 : tap // 3 + height, tap % 3 : tap % 3 + width] for tap in range(9)], 0
-    )
-
-
-def flip_stack(padded, height, width):
-    return jnp.concatenate(
-        [
-            padded[:, 2 - tap // 3 : 2 - tap // 3 + height, 2 - tap % 3 : 2 - tap % 3 + width]
-            for tap in range(9)
+        off = ((jpos < 2) & jnp.logical_not(left)) | ((jpos > 3) & jnp.logical_not(right))
+        off = off | ((hpos < 2) & jnp.logical_not(up)) | ((hpos > 17) & jnp.logical_not(down))
+        return jnp.where(off, 0.0, full)
+
+    def shifted(buf, count, ahead, edge):
+        def step(h, _):
+            x = buf[h, 1].astype(f32)
+            at = (h + ahead) * 6
+            before = pltpu.roll(x, 1, 1)
+            first = pltpu.roll(edge, 127 - at, 1)
+            buf[h, 0, :, :128] = jnp.where(lane == 0, first, before[:, :128]).astype(bf16)
+            buf[h, 0, :, 128:] = before[:, 128:].astype(bf16)
+            after = pltpu.roll(x, 255, 1)
+            last = pltpu.roll(edge, 123 - at, 1)
+            buf[h, 2, :, :128] = after[:, :128].astype(bf16)
+            buf[h, 2, :, 128:] = jnp.where(lane == 127, last, after[:, 128:]).astype(bf16)
+            return 0
+
+        lax.fori_loop(0, count, step, 0)
+
+    def window(buf, h):
+        return buf[pl.ds(h, 3)].reshape(864, 256)
+
+    feat_copy.wait()
+
+    def features(i, _):
+        at = pl.multiple_of(i * 16, 16)
+        xh[2:18, 1, pl.ds(at, 16), :] = jnp.swapaxes(fv[pl.ds(at, 16)], 0, 1)
+        return 0
+
+    lax.fori_loop(0, 6, features, 0)
+    tile[0] = own_tile(lambda h: xh[h + 2, 1]).astype(bf16)
+    pl.semaphore_wait(barrier, 8)
+    first = exchange(0, xh.at[2:4, 1], xh.at[16:18, 1], xh.at[0:2, 1], xh.at[18:20, 1])
+
+    def relayout(i, _):
+        at = pl.multiple_of(i * 16, 16)
+        t2[:, pl.ds(at, 16), :] = jnp.swapaxes(tin[pl.ds(at, 16)], 0, 1)
+        return 0
+
+    for k, c in enumerate(t_copies):
+        c.wait()
+        lax.fori_loop(k * (CHUNK // 16), (k + 1) * (CHUNK // 16), relayout, 0)
+    p = proj[...]
+    lhs[...] = jnp.concatenate([-p] + pieces(dot_nt(p, p)), axis=1)
+    v[...] = jnp.zeros_like(v)
+    gacc[...] = jnp.zeros_like(gacc)
+
+    for c in first:
+        c.wait_recv()
+
+    @pl.when(jnp.logical_not(up))
+    def _():
+        xh[0:2, 1] = jnp.zeros((2, 96, 256), bf16)
+
+    @pl.when(jnp.logical_not(down))
+    def _():
+        xh[18:20, 1] = jnp.zeros((2, 96, 256), bf16)
+
+    edge = rim(0)
+    shifted(xh, 20, 0, edge)
+
+    for t in range(9):
+        away = (t // 3 - 1) * 6 + t % 3 - 1
+        taps[t * 96 : (t + 1) * 96] = pltpu.roll(edge, (128 - away) % 128, 1).astype(bf16)
+    pre = dot(w1[...], taps[...])
+    side = (pre * phi(pre)).astype(bf16).astype(f32)
+    off = ((jpos < 2) & jnp.logical_not(left)) | ((jpos > 3) & jnp.logical_not(right))
+    off = off | ((hpos < 2) & jnp.logical_not(up)) | ((hpos > 17) & jnp.logical_not(down))
+    side = jnp.where(off, 0.0, side)
+
+    def conv1(r, _):
+        pre = dot(w1[...], window(xh, r))
+        cdf = phi(pre)
+        gp[r] = cdf + pre * (jnp.exp(-0.5 * pre * pre) * 0.3989422804014327)
+        outside = ((r == 0) & jnp.logical_not(up)) | ((r == 17) & jnp.logical_not(down))
+        hh[r, 1] = jnp.where(outside, 0.0, pre * cdf).astype(bf16)
+        return 0
+
+    lax.fori_loop(0, 18, conv1, 0)
+    shifted(hh, 18, 1, side)
+
+    def conv2(h, _):
+        s = (xh[h + 2, 1].astype(f32) + dot(w2[...], window(hh, h))).astype(bf16)
+        for k in range(3):
+            t2[h, 1536 + k * 96 : 1632 + k * 96] = s
+        ds[h + 1, 1] = (dot(lhs[...], t2[h]) * SCALE).astype(bf16)
+        return 0
+
+    lax.fori_loop(0, 16, conv2, 0)
+    tile[1] = own_tile(lambda h: ds[h + 1, 1]).astype(bf16)
+    second = exchange(1, ds.at[1, 1], ds.at[16, 1], ds.at[0, 1], ds.at[17, 1])
+
+    def grads(h, _):
+        gacc[:, :1632] += dot_nt(t2[h, 1536:1632], t2[h, :1632])
+        v[864:1728, :96] += dot_nt(window(hh, h), ds[h + 1, 1])
+        return 0
+
+    lax.fori_loop(0, 16, grads, 0)
+    mp = sum(dot(m, p) for m in pieces(gacc[:, 1536:1632]))
+    gp_out = (mp - gacc[:, :1536]) * SCALE
+    for k in range(12):
+        v[1728 + k * 96 : 1824 + k * 96] = gp_out[:, k * 128 : (k + 1) * 128]
+
+    for c in second:
+        c.wait_recv()
+
+    @pl.when(jnp.logical_not(up))
+    def _():
+        ds[0, 1] = jnp.zeros((96, 256), bf16)
+
+    @pl.when(jnp.logical_not(down))
+    def _():
+        ds[17, 1] = jnp.zeros((96, 256), bf16)
+
+    shifted(ds, 18, 1, rim(1))
+
+    def back(h, _):
+        dpre = (dot(wb[...], window(ds, h)) * gp[h + 1]).astype(bf16)
+        v[:864, :96] += dot_nt(window(xh, h + 1), dpre)
+        return 0
+
+    lax.fori_loop(0, 16, back, 0)
+    for c in first + second:
+        c.wait_send()
+
+
+def gradients(features, teacher, conv_in, conv_out, projector):
+    bf16, f32 = jnp.bfloat16, jnp.float32
+    w1 = conv_in.reshape(864, 96).T
+    w2 = conv_out.reshape(864, 96).T
+    wb = conv_out[::-1].transpose(1, 0, 2).reshape(96, 864)
+    vmem = pl.BlockSpec(memory_space=pltpu.VMEM)
+    hbm = pl.BlockSpec(memory_space=pl.ANY)
+    return pl.pallas_call(
+        main_kernel,
+        out_shape=jax.ShapeDtypeStruct((ROWS, 128), f32),
+        in_specs=[hbm, hbm, vmem, vmem, vmem, vmem],
+        out_specs=vmem,
+        scratch_shapes=[
+            pltpu.VMEM((96, 16, 256), bf16),
+            pltpu.VMEM((1536, 16, 256), bf16),
+            pltpu.VMEM((16, 1824, 256), bf16),
+            pltpu.VMEM((20, 3, 96, 256), bf16),
+            pltpu.VMEM((18, 3, 96, 256), bf16),
+            pltpu.VMEM((18, 96, 256), f32),
+            pltpu.VMEM((18, 3, 96, 256), bf16),
+            pltpu.VMEM((96, 1824), bf16),
+            pltpu.VMEM((96, 1664), f32),
+            pltpu.VMEM((864, 128), bf16),
+            pltpu.VMEM((2, 96, 128), bf16),
+            pltpu.VMEM((2, 8, 96, 128), bf16),
+            pltpu.SemaphoreType.DMA((7,)),
+            pltpu.SemaphoreType.DMA((2, 10)),
+            pltpu.SemaphoreType.DMA((2, 10)),
         ],
-        0,
-    )
+        compiler_params=pltpu.CompilerParams(
+            collective_id=0, has_side_effects=True, vmem_limit_bytes=60 * 2**20
+        ),
+    )(features, teacher, w1, w2, wb, projector)
 
 
 def shards(features, teacher, conv_in, conv_out, projector):
-    chans, height, width = features.shape
-    flat_in = conv_in.reshape(9 * chans, chans)
-    flat_out = conv_out.reshape(9 * chans, chans)
-    xpad = padded_2(features, (("row", 1), ("col", 2)), 1)
-    x_taps = tap_stack(xpad, height, width)
-    pre = jnp.einsum("ko,khw->ohw", flat_in, x_taps, preferred_element_type=jnp.float32)
-    hidden = jax.nn.gelu(pre, approximate=False).astype(jnp.bfloat16)
-    gpad = padded_2(hidden, (("row", 1), ("col", 2)), 1)
-    g_taps = tap_stack(gpad, height, width)
-    branch = jnp.einsum("ko,khw->ohw", flat_out, g_taps, preferred_element_type=jnp.float32)
-    student = (features.astype(jnp.float32) + branch).astype(jnp.bfloat16)
-    pred = jnp.einsum("ce,chw->ehw", projector, student, preferred_element_type=jnp.float32)
-    npix = height * width * lax.axis_size("row") * lax.axis_size("col")
-    dpred = ((pred - teacher.astype(jnp.float32)) / npix).astype(jnp.bfloat16)
-    grad_proj = jnp.einsum("chw,ehw->ce", student, dpred, preferred_element_type=jnp.float32)
-    dstudent = jnp.einsum(
-        "ce,ehw->chw", projector, dpred, preferred_element_type=jnp.float32
-    ).astype(jnp.bfloat16)
-    spad = padded_2(dstudent, (("row", 1), ("col", 2)), 1)
-    back_matrix = jnp.transpose(conv_out, (0, 2, 1)).reshape(9 * chans, chans)
-    dhidden = jnp.einsum(
-        "kc,khw->chw",
-        back_matrix,
-        flip_stack(spad, height, width),
-        preferred_element_type=jnp.float32,
-    )
-    dpre = (dhidden * gelu_grad(pre)).astype(jnp.bfloat16)
-    grad_out = jnp.einsum(
-        "khw,ohw->ko", g_taps, dstudent, preferred_element_type=jnp.float32
-    ).reshape(9, chans, chans)
-    grad_in = jnp.einsum("khw,ohw->ko", x_taps, dpre, preferred_element_type=jnp.float32).reshape(
-        9, chans, chans
-    )
-    flat = jnp.concatenate(
-        [
-            jnp.pad(grad_in.reshape(864, 96), ((0, 0), (0, 32))),
-            jnp.pad(grad_out.reshape(864, 96), ((0, 0), (0, 32))),
-            grad_proj.reshape(96, 12, 128).transpose(1, 0, 2).reshape(1152, 128),
-            jnp.zeros((192, 128), jnp.float32),
-        ]
-    )
-    return all_reduce(flat)
+    return all_reduce(gradients(features, teacher, conv_in, conv_out, projector))
 
 
 def solution(mesh):

time: 191 us -> 110 us (0.58)
  Pallas kernels: 49.5 us -> 100 us
  matrix products: 38.6 us -> 0 us
  starting transfers between devices: 37.2 us -> 0 us
  waiting for transfers between devices: 24.6 us -> 0 us
  local copies, waits for them, and re-layouts: 33.6 us -> 9.16 us
  other arithmetic: 5.48 us -> 0 us
    pallas_call x0 -> x1, Pallas kernels: none -> 58.6 us  [gradients(): pl.pallas_call(main_kernel, out_shape=jax.ShapeDtypeStruct((ROWS, 128), f...]
    dot_general x7 -> x0, matrix products: 38.6 us -> none  [the longest x1 9.21 us: shards(): jnp.einsum('ce,chw->ehw', projector, student, preferred_element_type=jnp....]
    ppermute x12 -> x0, starting transfers between devices: 37.2 us -> none  [the longest x6 26.9 us: padded_2(): lax.ppermute(tail, axis, [(i, (i + 1) % count) for i in range(ends)])]
    unnamed x44 -> x5, local copies, waits for them, and re-layouts: 29.7 us -> 3.74 us
    ppermute x12 -> x0, waiting for transfers between devices: 24.6 us -> none  [the longest x6 21 us: padded_2(): lax.ppermute(head, axis, [((i + 1) % count, i) for i in range(ends)])]
    pallas_call x1, Pallas kernels: 49.5 us -> 41.5 us  [all_reduce(): pl.pallas_call(reduce_kernel, out_shape=(jax.ShapeDtypeStruct((9, 96, 96)...]
    reshape x1 -> x3, local copies, waits for them, and re-layouts: 0.11 us -> 4.28 us  [the longest x1 1.73 us: gradients(): w1 = conv_in.reshape(864, 96).T]
    concatenate x6 -> x0, other arithmetic: 3.17 us -> none  [the longest x4 2.27 us: padded_2(): jnp.concatenate([lax.ppermute(tail, axis, [(i, (i + 1) % count) for i in...]
  transfers between devices with their start and end apart: 12 -> 0, of which waited for: 7 -> 0; matrix products, arithmetic and copies ran while one was open for 12% -> 0% of each run, Pallas kernels for 0% -> 0%
where the time goes in v2:
time: 110 us
  Pallas kernels  100 us (91%)
  local copies, waits for them, and re-layouts  9.16 us (8%)
    pallas_call x1, Pallas kernels, gradients(): pl.pallas_call(main_kernel, out_shape=jax.ShapeDtypeStruct((ROWS, 128), f...  58.6 us
    pallas_call x1, Pallas kernels, all_reduce(): pl.pallas_call(reduce_kernel, out_shape=(jax.ShapeDtypeStruct((9, 96, 96)...  41.5 us
    unnamed x5, local copies, waits for them, and re-layouts  3.74 us

profile of v2, /device:TPU:1, one launch (start us, length us, event | category | flops | bytes accessed | tf_op | source)
XLA Modules:
  0.0 109.9 jit_solution(94471801125630006)
XLA Ops:
  0.6 1.7 %copy.11 = bf16[864,96]{0,1:T(8,128)(2,1)} copy(bf16[864,96]{1,0:T(8,128)(2,1)} %bitcast.11) | data formatting | bytes 331776 | tf_op jit(solution)/shard_map/reshape | solution.py:436
  2.4 1.7 %copy.12 = bf16[864,96]{0,1:T(8,128)(2,1)} copy(bf16[864,96]{1,0:T(8,128)(2,1)} %bitcast.7) | data formatting | bytes 331776 | tf_op jit(solution)/shard_map/reshape | solution.py:437
  4.1 0.9 reverse_bitcast_fusion
  5.1 0.2 copy.13
  5.2 0.8 copy.14.wb
  6.0 58.6 %shard_map.76.v = f32[3072,128]{1,0:T(8,128)} custom-call(bf16[96,16,256]{2,1,0:T(8,128)(2,1)} %feat.1, bf16[1536,16,256]{2,1,0:T(8,128)(2,1)} %teach.1, bf16[96,864]{1,0:T(8,128)(2,1)} %bitcast.9, bf16[96,864]{1,0:T(8,128)(2,1)} %bitcast.10, bf16[96,864]{1,0:T(8,128)(2,1)} %copy.14.wb, bf16[96,1536]{1,0:T(8,128)(2,1)} %proj.1), custom_call_target="tpu_custom_call" | custom-call | tf_op jit(solution)/shard_map/pallas_call | solution.py:441
  64.6 0.0 copy-start
  64.6 1.4 %copy-done = f32[3072,128]{1,0:T(8,128)S(1)} copy-done((f32[3072,128]{1,0:T(8,128)S(1)}, f32[3072,128]{1,0:T(8,128)}, u32[]{:S(2)}) %copy-start) | copy-done | bytes 1572888
  66.0 41.5 %shard_map.77 = (f32[9,96,96]{2,1,0:T(8,128)S(1)}, f32[9,96,96]{2,1,0:T(8,128)S(1)}, f32[96,1536]{1,0:T(8,128)S(1)}) custom-call(f32[3072,128]{1,0:T(8,128)S(1)} %copy-done), custom_call_target="tpu_custom_call" | custom-call | tf_op jit(solution)/shard_map/pallas_call | solution.py:180
  107.6 0.8 copy.18
  108.3 0.8 copy.19
  109.1 0.8 copy.20
Async XLA Ops:
  64.6 1.4 %copy-start = (f32[3072,128]{1,0:T(8,128)S(1)}, f32[3072,128]{1,0:T(8,128)}, u32[]{:S(2)}) copy-start(f32[3072,128]{1,0:T(8,128)} %shard_map.76.v) | copy-start | bytes 4718596

commit v3 on v2

v3 whole, which is shorter than its diff:
```python
import jax
import jax.numpy as jnp
from jax import lax
from jax.experimental import pallas as pl
from jax.experimental.pallas import tpu as pltpu
from jax.sharding import PartitionSpec as P

MESH = pl.DeviceIdType.MESH
ROWS = 3072


def place():
    row, col = lax.axis_index("row"), lax.axis_index("col")
    return dict(x=(row % 2) * 2 + col // 8, y=(col // 2) % 4, z=row // 2, core=col % 2)


def device(at, **moved):
    p = dict(at, **moved)
    return (p["z"] * 2 + p["x"] // 2, ((p["x"] % 2) * 4 + p["y"]) * 2 + p["core"])


def peers(at):
    yield device(at, core=1 - at["core"])
    for axis, n in (("x", 4), ("y", 4), ("z", 8)):
        for step in range(1, n):
            yield device(at, **{axis: (at[axis] + step) % n})


def al(x):
    return pl.multiple_of(x, 8)


def reduce_rows(at, v, r, base, count, bufs, sent, got):
    w, in0, in1, in2, out3, in3, sums3 = bufs
    half, colour, big, small, unit = (count // k for k in (2, 4, 16, 64, 256))
    orders = (("x", "y"), ("y", "x"))
    copies = []

    def copy(src, dst, peer):
        k = len(copies)
        c = pltpu.make_async_remote_copy(
            src_ref=src,
            dst_ref=dst,
            send_sem=sent.at[k],
            recv_sem=got.at[k],
            device_id=peer,
            device_id_type=MESH,
        )
        c.start()
        copies.append(c)
        return c

    core, z = at["core"], at["z"]
    other = device(at, core=1 - core)
    mine = al(base + core * half)
    c = copy(v.at[pl.ds(al(base + (1 - core) * half), half)], in0, other)
    yield
    c.wait_recv()
    w[...] = v[pl.ds(mine, half)] + in0[...]

    def scatter(starts, axes, size, into):
        out = []
        for k in range(2):
            for step in range(1, 4):
                q = (at[axes[k]] + step) % 4
                rows = pl.ds(al(starts[k] + q * size), size)
                out.append(copy(w.at[rows], into.at[k, step - 1], device(at, **{axes[k]: q})))
        return out

    waits = scatter((0, colour), ("x", "y"), big, in1)
    yield
    starts = []
    for k, axis in enumerate(("x", "y")):
        for c in waits[3 * k : 3 * k + 3]:
            c.wait_recv()
        starts.append(al(k * colour + at[axis] * big))
        rows = pl.ds(starts[k], big)
        w[rows] = w[rows] + in1[k, 0] + in1[k, 1] + in1[k, 2]
    waits = scatter(starts, ("y", "x"), small, in2)
    yield
    smalls = []
    for k, axis in enumerate(("y", "x")):
        for c in waits[3 * k : 3 * k + 3]:
            c.wait_recv()
        smalls.append(al(starts[k] + at[axis] * small))
        total = w[pl.ds(smalls[k], small)] + in2[k, 0] + in2[k, 1] + in2[k, 2]
        out3[k * 4 : k * 4 + 4] = total.reshape(4, unit, 128)
    waits = []
    for step in range(1, 8):
        q = (z + step) % 8
        waits.append(copy(out3.at[q], in3.at[step - 1], device(at, z=q)))
    yield
    total = out3[z]
    for k, c in enumerate(waits):
        c.wait_recv()
        total = total + in3[k]
    sums3[z] = total
    waits = []
    for step in range(1, 8):
        q = (z + step) % 8
        waits.append(copy(sums3.at[z], sums3.at[z], device(at, z=q)))
    yield
    for c in waits:
        c.wait_recv()
    waits = []
    for k, axis in enumerate(("y", "x")):
        rows = pl.ds(al(mine + smalls[k]), small)
        r[rows] = sums3[k * 4 : k * 4 + 4].reshape(small, 128)
        for step in range(1, 4):
            q = (at[axis] + step) % 4
            waits.append(copy(r.at[rows], r.at[rows], device(at, **{axis: q})))
    yield
    for c in waits:
        c.wait_recv()
    waits = []
    last = []
    for k, axis in enumerate(("x", "y")):
        rows = pl.ds(al(mine + starts[k]), big)
        for step in range(1, 4):
            q = (at[axis] + step) % 4
            waits.append(copy(r.at[rows], r.at[rows], device(at, **{axis: q})))
        last.append(copy(r.at[rows], r.at[rows], other))
    yield
    for k, axis in enumerate(("x", "y")):
        for step in range(1, 4):
            q = (at[axis] - step + 4) % 4
            rows = pl.ds(al(mine + k * colour + q * big), big)
            waits[3 * k + step - 1].wait_recv()
            last.append(copy(r.at[rows], r.at[rows], other))
    yield
    for c in last:
        c.wait_recv()
    for c in copies:
        c.wait_send()


def reduce_scratch(count):
    half, colour, big, small, unit = (count // k for k in (2, 4, 16, 64, 256))
    f32 = jnp.float32
    return [
        pltpu.VMEM((half, 128), f32),
        pltpu.VMEM((half, 128), f32),
        pltpu.VMEM((2, 3, big, 128), f32),
        pltpu.VMEM((2, 3, small, 128), f32),
        pltpu.VMEM((8, unit, 128), f32),
        pltpu.VMEM((7, unit, 128), f32),
        pltpu.VMEM((8, unit, 128), f32),
    ]


AROUND = ((-1, 0), (1, 0), (0, -1), (0, 1), (-1, -1), (-1, 1), (1, -1), (1, 1))
SCALE = 2.0**-20
CHUNK = 256


def dot(a, b):
    return jnp.dot(a, b, preferred_element_type=jnp.float32)


def dot_nt(a, b):
    return lax.dot_general(a, b, (((1,), (1,)), ((), ())), preferred_element_type=jnp.float32)


def pieces(value):
    out = []
    for _ in range(3):
        out.append(value.astype(jnp.bfloat16))
        value = value - out[-1].astype(jnp.float32)
    return out


def phi(value):
    return 0.5 * (1.0 + lax.erf(value * 0.7071067811865476))


def main_kernel(
    feat, teach, cin, cout, proj, gin, gout, gproj, v, r, sent_sum, got_sum,
    a0, a1, a2, a3, a4, a5, a6, b0, b1, b2, b3, b4, b5, b6,
    fv, cv, dv, p, tin, t2, xh, hh, gp, ds, w1, w2, wb, lhs, gacc, taps, tile, around, local, sent, got,
):
    bf16, f32 = jnp.bfloat16, jnp.float32
    rows, cols = lax.axis_size("row"), lax.axis_size("col")
    row, col = lax.axis_index("row"), lax.axis_index("col")
    up, down, left, right = row > 0, row < rows - 1, col > 0, col < cols - 1

    def neighbour(dr, dc):
        return ((row + dr + rows) % rows, (col + dc + cols) % cols)

    feat_copy = pltpu.make_async_copy(feat, fv, local.at[0])
    feat_copy.start()
    small = []
    for k, (src, dst) in enumerate(((cin, cv), (cout, dv), (proj, p))):
        small.append(pltpu.make_async_copy(src, dst, local.at[k + 7]))
        small[-1].start()
    t_copies = []
    for k in range(1536 // CHUNK):
        part = pl.ds(k * CHUNK, CHUNK)
        t_copies.append(pltpu.make_async_copy(teach.at[part], tin.at[part], local.at[k + 1]))
        t_copies[-1].start()
    barrier = pltpu.get_barrier_semaphore()
    place_here = place()
    greeted = [neighbour(dr, dc) for dr, dc in AROUND] + list(peers(place_here))
    for peer in greeted:
        pl.semaphore_signal(barrier, inc=1, device_id=peer, device_id_type=MESH)

    lane = lax.broadcasted_iota(jnp.int32, (96, 128), 1)
    hpos = (lane * 43) >> 8
    jpos = lane - hpos * 6

    def own_tile(read):
        acc = jnp.zeros((96, 128), f32)
        for h in range(16):
            x = read(h).astype(f32)
            at = (h + 2) * 6
            here = hpos == h + 2
            acc = jnp.where(here & (jpos < 2), pltpu.roll(x[:, 128:], at + 2, 1), acc)
            acc = jnp.where(here & (jpos > 3), pltpu.roll(x[:, :128], at + 4, 1), acc)
        return acc

    def exchange(part, top, bottom, to_top, to_bottom):
        copies = []

        def send(k, src, dst, dr, dc):
            c = pltpu.make_async_remote_copy(
                src_ref=src,
                dst_ref=dst,
                send_sem=sent.at[part, k],
                recv_sem=got.at[part, k],
                device_id=neighbour(dr, dc),
                device_id_type=MESH,
            )
            c.start()
            copies.append(c)

        send(8, top, to_bottom, -1, 0)
        send(9, bottom, to_top, 1, 0)
        for k, (dr, dc) in enumerate(AROUND):
            send(k, tile.at[part], around.at[part, AROUND.index((-dr, -dc))], dr, dc)
        return copies

    def rim(part):
        def get(dr, dc):
            if (dr, dc) == (0, 0):
                return tile[part].astype(f32)
            return around[part, AROUND.index((dr, dc))].astype(f32)

        def band(dr):
            mid = get(dr, 0)
            inner = jnp.where(jpos == 2, pltpu.roll(mid, 126, 1), pltpu.roll(mid, 2, 1))
            outer = jnp.where(jpos < 2, get(dr, -1), get(dr, 1))
            return jnp.where((jpos == 2) | (jpos == 3), inner, outer)

        full = jnp.where(
            hpos < 2,
            pltpu.roll(band(-1), 32, 1),
            jnp.where(hpos < 18, band(0), pltpu.roll(band(1), 96, 1)),
        )
        off = ((jpos < 2) & jnp.logical_not(left)) | ((jpos > 3) & jnp.logical_not(right))
        off = off | ((hpos < 2) & jnp.logical_not(up)) | ((hpos > 17) & jnp.logical_not(down))
        return jnp.where(off, 0.0, full)

    def shifted(buf, count, ahead, edge):
        def step(h, _):
            x = buf[h, 1].astype(f32)
            at = (h + ahead) * 6
            before = pltpu.roll(x, 1, 1)
            first = pltpu.roll(edge, 127 - at, 1)
            buf[h, 0, :, :128] = jnp.where(lane == 0, first, before[:, :128]).astype(bf16)
            buf[h, 0, :, 128:] = before[:, 128:].astype(bf16)
            after = pltpu.roll(x, 255, 1)
            last = pltpu.roll(edge, 123 - at, 1)
            buf[h, 2, :, :128] = after[:, :128].astype(bf16)
            buf[h, 2, :, 128:] = jnp.where(lane == 127, last, after[:, 128:]).astype(bf16)
            return 0

        lax.fori_loop(0, count, step, 0, unroll=2)

    def window(buf, h):
        return buf[pl.ds(h, 3)].reshape(864, 256)

    feat_copy.wait()

    def features(i, _):
        at = pl.multiple_of(i * 16, 16)
        xh[2:18, 1, pl.ds(at, 16), :] = jnp.swapaxes(fv[pl.ds(at, 16)], 0, 1)
        return 0

    lax.fori_loop(0, 6, features, 0)
    tile[0] = own_tile(lambda h: xh[h + 2, 1]).astype(bf16)
    pl.semaphore_wait(barrier, len(greeted))
    first = exchange(0, xh.at[2:4, 1], xh.at[16:18, 1], xh.at[0:2, 1], xh.at[18:20, 1])

    def relayout(i, _):
        at = pl.multiple_of(i * 16, 16)
        t2[:, pl.ds(at, 16), :] = jnp.swapaxes(tin[pl.ds(at, 16)], 0, 1)
        return 0

    for k, c in enumerate(t_copies):
        c.wait()
        lax.fori_loop(k * (CHUNK // 16), (k + 1) * (CHUNK // 16), relayout, 0)
    for c in small:
        c.wait()
    for dst, src in ((w1, cv), (w2, dv)):
        dst[...] = jnp.concatenate([src[t].astype(f32).T.astype(bf16) for t in range(9)], axis=1)
    wb[...] = jnp.concatenate([dv[8 - t] for t in range(9)], axis=1)
    lhs[...] = jnp.concatenate([-p[...]] + pieces(dot_nt(p[...], p[...])), axis=1)
    v[...] = jnp.zeros_like(v)
    gacc[...] = jnp.zeros_like(gacc)

    for c in first:
        c.wait_recv()

    @pl.when(jnp.logical_not(up))
    def _():
        xh[0:2, 1] = jnp.zeros((2, 96, 256), bf16)

    @pl.when(jnp.logical_not(down))
    def _():
        xh[18:20, 1] = jnp.zeros((2, 96, 256), bf16)

    edge = rim(0)
    shifted(xh, 20, 0, edge)

    for t in range(9):
        away = (t // 3 - 1) * 6 + t % 3 - 1
        taps[t * 96 : (t + 1) * 96] = pltpu.roll(edge, (128 - away) % 128, 1).astype(bf16)
    pre = dot(w1[...], taps[...])
    side = (pre * phi(pre)).astype(bf16).astype(f32)
    off = ((jpos < 2) & jnp.logical_not(left)) | ((jpos > 3) & jnp.logical_not(right))
    off = off | ((hpos < 2) & jnp.logical_not(up)) | ((hpos > 17) & jnp.logical_not(down))
    side = jnp.where(off, 0.0, side)

    def conv1(r, _):
        pre = dot(w1[...], window(xh, r))
        cdf = phi(pre)
        gp[r] = cdf + pre * (jnp.exp(-0.5 * pre * pre) * 0.3989422804014327)
        outside = ((r == 0) & jnp.logical_not(up)) | ((r == 17) & jnp.logical_not(down))
        hh[r, 1] = jnp.where(outside, 0.0, pre * cdf).astype(bf16)
        return 0

    lax.fori_loop(0, 18, conv1, 0, unroll=3)
    shifted(hh, 18, 1, side)

    def conv2(h, _):
        s = (xh[h + 2, 1].astype(f32) + dot(w2[...], window(hh, h))).astype(bf16)
        for k in range(3):
            t2[h, 1536 + k * 96 : 1632 + k * 96] = s
        ds[h + 1, 1] = (dot(lhs[...], t2[h]) * SCALE).astype(bf16)
        return 0

    lax.fori_loop(0, 16, conv2, 0, unroll=2)
    tile[1] = own_tile(lambda h: ds[h + 1, 1]).astype(bf16)
    second = exchange(1, ds.at[1, 1], ds.at[16, 1], ds.at[0, 1], ds.at[17, 1])

    def wide(read, h):
        return jnp.concatenate([read(h * 4 + k) for k in range(4)], axis=1)

    def grads(h, _):
        gacc[:, :96] += dot_nt(
            wide(lambda k: t2[k, :1632], h), wide(lambda k: t2[k, 1536:1632], h)
        )
        return 0

    def grads_out(h, _):
        v[:864, :96] += dot_nt(wide(lambda k: window(hh, k), h), wide(lambda k: ds[k + 1, 1], h))
        return 0

    lax.fori_loop(0, 4, grads, 0)
    mp = sum(dot(m, p[...]) for m in pieces(gacc[1536:1632, :96]))
    for k in range(12):
        part = slice(k * 128, (k + 1) * 128)
        v[864 + k * 96 : 960 + k * 96] = (mp[:, part] - gacc[part].T[:96]) * SCALE
    lax.fori_loop(0, 4, grads_out, 0)
    early = reduce_rows(
        place_here, v, r, 0, 2048, (a0, a1, a2, a3, a4, a5, a6), sent_sum.at[0], got_sum.at[0]
    )
    late = reduce_rows(
        place_here, v, r, 2048, 1024, (b0, b1, b2, b3, b4, b5, b6), sent_sum.at[1], got_sum.at[1]
    )
    next(early)

    for c in second:
        c.wait_recv()

    @pl.when(jnp.logical_not(up))
    def _():
        ds[0, 1] = jnp.zeros((96, 256), bf16)

    @pl.when(jnp.logical_not(down))
    def _():
        ds[17, 1] = jnp.zeros((96, 256), bf16)

    shifted(ds, 18, 1, rim(1))

    def back(h, _):
        def dpre(k):
            return (dot(wb[...], window(ds, k)) * gp[k + 1]).astype(bf16)

        v[2048:2912, :96] += dot_nt(wide(lambda k: window(xh, k + 1), h), wide(dpre, h))
        return 0

    next(early)
    lax.fori_loop(0, 2, back, 0)
    next(early)
    lax.fori_loop(2, 4, back, 0)
    next(late)
    for _ in range(5):
        next(early, None)
        next(late, None)
    next(early, None)
    for t in range(9):
        gout[t] = r[t * 96 : (t + 1) * 96, :96]
    for t in range(12):
        gproj[:, t * 128 : (t + 1) * 128] = r[864 + t * 96 : 960 + t * 96]
    for _ in late:
        pass
    for t in range(9):
        gin[t] = r[2048 + t * 96 : 2144 + t * 96, :96]
    for c in first + second:
        c.wait_send()


def gradients(features, teacher, conv_in, conv_out, projector):
    bf16, f32 = jnp.bfloat16, jnp.float32
    vmem = pl.BlockSpec(memory_space=pltpu.VMEM)
    hbm = pl.BlockSpec(memory_space=pl.ANY)
    return pl.pallas_call(
        main_kernel,
        out_shape=(
            jax.ShapeDtypeStruct((9, 96, 96), f32),
            jax.ShapeDtypeStruct((9, 96, 96), f32),
            jax.ShapeDtypeStruct((96, 1536), f32),
        ),
        in_specs=[hbm] * 5,
        out_specs=(vmem, vmem, vmem),
        scratch_shapes=[
            pltpu.VMEM((ROWS, 128), f32),
            pltpu.VMEM((ROWS, 128), f32),
            pltpu.SemaphoreType.DMA((2, 48)),
            pltpu.SemaphoreType.DMA((2, 48)),
            *reduce_scratch(2048),
            *reduce_scratch(1024),
            pltpu.VMEM((96, 16, 256), bf16),
            pltpu.VMEM((9, 96, 96), bf16),
            pltpu.VMEM((9, 96, 96), bf16),
            pltpu.VMEM((96, 1536), bf16),
            pltpu.VMEM((1536, 16, 256), bf16),
            pltpu.VMEM((16, 1824, 256), bf16),
            pltpu.VMEM((20, 3, 96, 256), bf16),
            pltpu.VMEM((18, 3, 96, 256), bf16),
            pltpu.VMEM((18, 96, 256), f32),
            pltpu.VMEM((18, 3, 96, 256), bf16),
            pltpu.VMEM((96, 864), bf16),
            pltpu.VMEM((96, 864), bf16),
            pltpu.VMEM((96, 864), bf16),
            pltpu.VMEM((96, 1824), bf16),
            pltpu.VMEM((1632, 128), f32),
            pltpu.VMEM((864, 128), bf16),
            pltpu.VMEM((2, 96, 128), bf16),
            pltpu.VMEM((2, 8, 96, 128), bf16),
            pltpu.SemaphoreType.DMA((10,)),
            pltpu.SemaphoreType.DMA((2, 10)),
            pltpu.SemaphoreType.DMA((2, 10)),
        ],
        compiler_params=pltpu.CompilerParams(
            collective_id=0, has_side_effects=True, vmem_limit_bytes=63 * 2**20
        ),
    )(features, teacher, conv_in, conv_out, projector)


def solution(mesh):
    in_specs = (P(None, "row", "col"), P(None, "row", "col"), P(), P(), P())
    out_specs = (P(), P(), P())
    return jax.shard_map(gradients, mesh=mesh, in_specs=in_specs, out_specs=out_specs, check_vma=False)
```

time: 110 us -> 88 us (0.80)
  Pallas kernels: 100 us -> 81.6 us
  local copies, waits for them, and re-layouts: 9.16 us -> 5.52 us
    pallas_call x2 -> x1, Pallas kernels: 100 us -> 81.6 us  [gradients(): pl.pallas_call(main_kernel, out_shape=(jax.ShapeDtypeStruct((9, 96, 96),...]
    reshape x3 -> x0, local copies, waits for them, and re-layouts: 4.28 us -> none  [the longest x1 1.73 us: gradients(): w1 = conv_in.reshape(864, 96).T]
    unnamed x5 -> x3, local copies, waits for them, and re-layouts: 3.74 us -> 5.52 us
    transpose x2 -> x0, local copies, waits for them, and re-layouts: 1.13 us -> none  [gradients(): wb = conv_out[::-1].transpose(1, 0, 2).reshape(96, 864)]
where the time goes in v3:
time: 88 us; the launch traced here: 87.8 us
  Pallas kernels  81.6 us (93%)
  local copies, waits for them, and re-layouts  5.52 us (6%)
    pallas_call x1, Pallas kernels, gradients(): pl.pallas_call(main_kernel, out_shape=(jax.ShapeDtypeStruct((9, 96, 96),...  81.6 us
    unnamed x3, local copies, waits for them, and re-layouts  5.52 us

profile of v3, /device:TPU:1, one launch (start us, length us, event | category | flops | bytes accessed | tf_op | source)
XLA Modules:
  0.0 87.8 jit_solution(413093205683972757)
XLA Ops:
  0.6 81.6 %shard_map.76 = (f32[9,96,96]{2,1,0:T(8,128)}, f32[9,96,96]{2,1,0:T(8,128)}, f32[96,1536]{1,0:T(8,128)}) custom-call(bf16[96,16,256]{2,1,0:T(8,128)(2,1)} %feat.1, bf16[1536,16,256]{2,1,0:T(8,128)(2,1)} %teach.1, bf16[9,96,96]{2,1,0:T(8,128)(2,1)} %cin.1, bf16[9,96,96]{2,1,0:T(8,128)(2,1)} %cout.1, bf16[96,1536]{1,0:T(8,128)(2,1)} %proj.1), custom_call_target="tpu_custom_call" | custom-call | tf_op jit(solution)/shard_map/pallas_call | solution.py:427
  82.2 1.8 %copy.11 = f32[9,96,96]{2,1,0:T(8,128)} copy(f32[9,96,96]{2,1,0:T(8,128)} %get-tuple-element.6) | data formatting | bytes 663552
  84.0 1.8 %copy.12 = f32[9,96,96]{2,1,0:T(8,128)} copy(f32[9,96,96]{2,1,0:T(8,128)} %get-tuple-element.7) | data formatting | bytes 663552
  85.8 1.9 %copy.13 = f32[96,1536]{1,0:T(8,128)} copy(f32[96,1536]{1,0:T(8,128)} %get-tuple-element.8) | data formatting | bytes 1179648

commit v4 on v3

--- a/solution.py
+++ b/solution.py
@@ -174,8 +174,8 @@
 
 
 def main_kernel(
-    feat, teach, cin, cout, proj, gin, gout, gproj, v, r, sent_sum, got_sum,
-    a0, a1, a2, a3, a4, a5, a6, b0, b1, b2, b3, b4, b5, b6,
+    feat, teach, cin, cout, proj, r, v, sent_sum, got_sum,
+    a0, a1, a2, a3, a4, a5, a6, b0, b1, b2, b3, b4, b5, b6, c0, c1, c2, c3, c4, c5, c6,
     fv, cv, dv, p, tin, t2, xh, hh, gp, ds, w1, w2, wb, lhs, gacc, taps, tile, around, local, sent, got,
 ):
     bf16, f32 = jnp.bfloat16, jnp.float32
@@ -204,22 +204,22 @@
         pl.semaphore_signal(barrier, inc=1, device_id=peer, device_id_type=MESH)
 
     lane = lax.broadcasted_iota(jnp.int32, (96, 128), 1)
-    hpos = (lane * 43) >> 8
-    jpos = lane - hpos * 6
+    hpos = (((lane + 2) * 43) >> 8) - 1
+    jpos = lane - 4 - hpos * 6
+    off = ((jpos < 2) & jnp.logical_not(left)) | ((jpos > 3) & jnp.logical_not(right))
+    off = off | ((hpos < 2) & jnp.logical_not(up)) | ((hpos > 17) & jnp.logical_not(down))
 
     def own_tile(read):
         acc = jnp.zeros((96, 128), f32)
         for h in range(16):
             x = read(h).astype(f32)
-            at = (h + 2) * 6
+            at = (h + 2) * 6 + 4
             here = hpos == h + 2
             acc = jnp.where(here & (jpos < 2), pltpu.roll(x[:, 128:], at + 2, 1), acc)
             acc = jnp.where(here & (jpos > 3), pltpu.roll(x[:, :128], at + 4, 1), acc)
-        return acc
+        return jnp.concatenate([acc, jnp.zeros((32, 128), f32)]).T.astype(bf16)
 
     def exchange(part, top, bottom, to_top, to_bottom):
-        copies = []
-
         def send(k, src, dst, dr, dc):
             c = pltpu.make_async_remote_copy(
                 src_ref=src,
@@ -230,50 +230,61 @@
                 device_id_type=MESH,
             )
             c.start()
-            copies.append(c)
-
-        send(8, top, to_bottom, -1, 0)
-        send(9, bottom, to_top, 1, 0)
-        for k, (dr, dc) in enumerate(AROUND):
-            send(k, tile.at[part], around.at[part, AROUND.index((-dr, -dc))], dr, dc)
-        return copies
-
-    def rim(part):
-        def get(dr, dc):
-            if (dr, dc) == (0, 0):
-                return tile[part].astype(f32)
-            return around[part, AROUND.index((dr, dc))].astype(f32)
-
-        def band(dr):
-            mid = get(dr, 0)
-            inner = jnp.where(jpos == 2, pltpu.roll(mid, 126, 1), pltpu.roll(mid, 2, 1))
-            outer = jnp.where(jpos < 2, get(dr, -1), get(dr, 1))
-            return jnp.where((jpos == 2) | (jpos == 3), inner, outer)
-
-        full = jnp.where(
-            hpos < 2,
-            pltpu.roll(band(-1), 32, 1),
-            jnp.where(hpos < 18, band(0), pltpu.roll(band(1), 96, 1)),
-        )
-        off = ((jpos < 2) & jnp.logical_not(left)) | ((jpos > 3) & jnp.logical_not(right))
-        off = off | ((hpos < 2) & jnp.logical_not(up)) | ((hpos > 17) & jnp.logical_not(down))
+            return c
+
+        def send_tile(k):
+            dr, dc = AROUND[k]
+            lines = (slice(16, 112), slice(96, 112), slice(16, 32))[dr]
+            return send(
+                k,
+                tile.at[part, lines],
+                around.at[part, AROUND.index((-dr, -dc)), lines],
+                dr,
+                dc,
+            )
+
+        sides = [send_tile(2), send_tile(3)]
+        rest = [send(8, top, to_bottom, -1, 0), send(9, bottom, to_top, 1, 0)]
+        rest += [send_tile(k) for k in (0, 1, 4, 5, 6, 7)]
+        return sides, rest
+
+    def rim(part, whole):
+        def column(dc):
+            def piece(dr, lines):
+                if (dr, dc) == (0, 0):
+                    return tile[part, lines]
+                return around[part, AROUND.index((dr, dc)), lines]
+
+            above = below = jnp.zeros((16, 128), bf16)
+            if whole:
+                above, below = piece(-1, slice(96, 112)), piece(1, slice(16, 32))
+            lines = jnp.concatenate([above, piece(0, slice(16, 112)), below])
+            return lines.astype(f32).T[:96]
+
+        mid = column(0)
+        inner = jnp.where(jpos == 2, pltpu.roll(mid, 126, 1), pltpu.roll(mid, 2, 1))
+        outer = jnp.where(jpos < 2, column(-1), column(1))
+        full = jnp.where((jpos == 2) | (jpos == 3), inner, outer)
         return jnp.where(off, 0.0, full)
 
-    def shifted(buf, count, ahead, edge):
+    def shift_row(buf, h, ahead, edge):
+        x = buf[h, 1].astype(f32)
+        at = (h + ahead) * 6
+        before = pltpu.roll(x, 1, 1)
+        first = pltpu.roll(edge, 123 - at, 1)
+        buf[h, 0, :, :128] = jnp.where(lane == 0, first, before[:, :128]).astype(bf16)
+        buf[h, 0, :, 128:] = before[:, 128:].astype(bf16)
+        after = pltpu.roll(x, 255, 1)
+        last = pltpu.roll(edge, 119 - at, 1)
+        buf[h, 2, :, :128] = after[:, :128].astype(bf16)
+        buf[h, 2, :, 128:] = jnp.where(lane == 127, last, after[:, 128:]).astype(bf16)
+
+    def shifted(buf, start, stop, ahead, edge):
         def step(h, _):
-            x = buf[h, 1].astype(f32)
-            at = (h + ahead) * 6
-            before = pltpu.roll(x, 1, 1)
-            first = pltpu.roll(edge, 127 - at, 1)
-            buf[h, 0, :, :128] = jnp.where(lane == 0, first, before[:, :128]).astype(bf16)
-            buf[h, 0, :, 128:] = before[:, 128:].astype(bf16)
-            after = pltpu.roll(x, 255, 1)
-            last = pltpu.roll(edge, 123 - at, 1)
-            buf[h, 2, :, :128] = after[:, :128].astype(bf16)
-            buf[h, 2, :, 128:] = jnp.where(lane == 127, last, after[:, 128:]).astype(bf16)
+            shift_row(buf, h, ahead, edge)
             return 0
 
-        lax.fori_loop(0, count, step, 0, unroll=2)
+        lax.fori_loop(start, stop, step, 0, unroll=2)
 
     def window(buf, h):
         return buf[pl.ds(h, 3)].reshape(864, 256)
@@ -286,9 +297,9 @@
         return 0
 
     lax.fori_loop(0, 6, features, 0)
-    tile[0] = own_tile(lambda h: xh[h + 2, 1]).astype(bf16)
+    tile[0] = own_tile(lambda h: xh[h + 2, 1])
     pl.semaphore_wait(barrier, len(greeted))
-    first = exchange(0, xh.at[2:4, 1], xh.at[16:18, 1], xh.at[0:2, 1], xh.at[18:20, 1])
+    first_sides, first = exchange(0, xh.at[2:4, 1], xh.at[16:18, 1], xh.at[0:2, 1], xh.at[18:20, 1])
 
     def relayout(i, _):
         at = pl.multiple_of(i * 16, 16)
@@ -307,29 +318,6 @@
     v[...] = jnp.zeros_like(v)
     gacc[...] = jnp.zeros_like(gacc)
 
-    for c in first:
-        c.wait_recv()
-
-    @pl.when(jnp.logical_not(up))
-    def _():
-        xh[0:2, 1] = jnp.zeros((2, 96, 256), bf16)
-
-    @pl.when(jnp.logical_not(down))
-    def _():
-        xh[18:20, 1] = jnp.zeros((2, 96, 256), bf16)
-
-    edge = rim(0)
-    shifted(xh, 20, 0, edge)
-
-    for t in range(9):
-        away = (t // 3 - 1) * 6 + t % 3 - 1
-        taps[t * 96 : (t + 1) * 96] = pltpu.roll(edge, (128 - away) % 128, 1).astype(bf16)
-    pre = dot(w1[...], taps[...])
-    side = (pre * phi(pre)).astype(bf16).astype(f32)
-    off = ((jpos < 2) & jnp.logical_not(left)) | ((jpos > 3) & jnp.logical_not(right))
-    off = off | ((hpos < 2) & jnp.logical_not(up)) | ((hpos > 17) & jnp.logical_not(down))
-    side = jnp.where(off, 0.0, side)
-
     def conv1(r, _):
         pre = dot(w1[...], window(xh, r))
         cdf = phi(pre)
@@ -338,8 +326,34 @@
         hh[r, 1] = jnp.where(outside, 0.0, pre * cdf).astype(bf16)
         return 0
 
-    lax.fori_loop(0, 18, conv1, 0, unroll=3)
-    shifted(hh, 18, 1, side)
+    for c in first_sides:
+        c.wait_recv()
+    shifted(xh, 2, 18, 0, rim(0, False))
+    lax.fori_loop(2, 16, conv1, 0, unroll=2)
+
+    for c in first:
+        c.wait_recv()
+
+    @pl.when(jnp.logical_not(up))
+    def _():
+        xh[0:2, 1] = jnp.zeros((2, 96, 256), bf16)
+
+    @pl.when(jnp.logical_not(down))
+    def _():
+        xh[18:20, 1] = jnp.zeros((2, 96, 256), bf16)
+
+    edge = rim(0, True)
+    for h in (0, 1, 18, 19):
+        shift_row(xh, h, 0, edge)
+    for line in (0, 1, 16, 17):
+        conv1(line, 0)
+
+    for t in range(9):
+        away = (t // 3 - 1) * 6 + t % 3 - 1
+        taps[t * 96 : (t + 1) * 96] = pltpu.roll(edge, (128 - away) % 128, 1).astype(bf16)
+    pre = dot(w1[...], taps[...])
+    side = jnp.where(off, 0.0, (pre * phi(pre)).astype(bf16).astype(f32))
+    shifted(hh, 0, 18, 1, side)
 
     def conv2(h, _):
         s = (xh[h + 2, 1].astype(f32) + dot(w2[...], window(hh, h))).astype(bf16)
@@ -349,8 +363,8 @@
         return 0
 
     lax.fori_loop(0, 16, conv2, 0, unroll=2)
-    tile[1] = own_tile(lambda h: ds[h + 1, 1]).astype(bf16)
-    second = exchange(1, ds.at[1, 1], ds.at[16, 1], ds.at[0, 1], ds.at[17, 1])
+    tile[1] = own_tile(lambda h: ds[h + 1, 1])
+    second_sides, second = exchange(1, ds.at[1, 1], ds.at[16, 1], ds.at[0, 1], ds.at[17, 1])
 
     def wide(read, h):
         return jnp.concatenate([read(h * 4 + k) for k in range(4)], axis=1)
@@ -362,24 +376,29 @@
         return 0
 
     def grads_out(h, _):
-        v[:864, :96] += dot_nt(wide(lambda k: window(hh, k), h), wide(lambda k: ds[k + 1, 1], h))
+        v[1152:2016, :96] += dot_nt(wide(lambda k: window(hh, k), h), wide(lambda k: ds[k + 1, 1], h))
         return 0
 
     lax.fori_loop(0, 4, grads, 0)
     mp = sum(dot(m, p[...]) for m in pieces(gacc[1536:1632, :96]))
     for k in range(12):
         part = slice(k * 128, (k + 1) * 128)
-        v[864 + k * 96 : 960 + k * 96] = (mp[:, part] - gacc[part].T[:96]) * SCALE
-    lax.fori_loop(0, 4, grads_out, 0)
-    early = reduce_rows(
-        place_here, v, r, 0, 2048, (a0, a1, a2, a3, a4, a5, a6), sent_sum.at[0], got_sum.at[0]
-    )
-    late = reduce_rows(
-        place_here, v, r, 2048, 1024, (b0, b1, b2, b3, b4, b5, b6), sent_sum.at[1], got_sum.at[1]
-    )
-    next(early)
-
-    for c in second:
+        v[k * 96 : 96 + k * 96] = (mp[:, part] - gacc[part].T[:96]) * SCALE
+    sums = {
+        name: reduce_rows(
+            place_here, v, r, k * 1024, 1024, bufs, sent_sum.at[k], got_sum.at[k]
+        )
+        for k, (name, bufs) in enumerate(
+            (
+                ("E", (a0, a1, a2, a3, a4, a5, a6)),
+                ("M", (b0, b1, b2, b3, b4, b5, b6)),
+                ("L", (c0, c1, c2, c3, c4, c5, c6)),
+            )
+        )
+    }
+    next(sums["E"])
+
+    for c in second_sides + second:
         c.wait_recv()
 
     @pl.when(jnp.logical_not(up))
@@ -390,7 +409,7 @@
     def _():
         ds[17, 1] = jnp.zeros((96, 256), bf16)
 
-    shifted(ds, 18, 1, rim(1))
+    shifted(ds, 0, 18, 1, rim(1, True))
 
     def back(h, _):
         def dpre(k):
@@ -399,46 +418,47 @@
         v[2048:2912, :96] += dot_nt(wide(lambda k: window(xh, k + 1), h), wide(dpre, h))
         return 0
 
-    next(early)
-    lax.fori_loop(0, 2, back, 0)
-    next(early)
-    lax.fori_loop(2, 4, back, 0)
-    next(late)
-    for _ in range(5):
-        next(early, None)
-        next(late, None)
-    next(early, None)
+    next(sums["E"])
+    lax.fori_loop(0, 4, back, 0)
+    next(sums["L"])
+    next(sums["E"])
+    lax.fori_loop(0, 2, grads_out, 0)
+    next(sums["L"])
+    lax.fori_loop(2, 4, grads_out, 0)
+    for name in "MEMLEMLMELEMLEMLEM":
+        next(sums[name], None)
+    for _ in sums["L"]:
+        pass
+    for name in "EM":
+        for _ in sums[name]:
+            pass
+    for c in first_sides + first + second_sides + second:
+        c.wait_send()
+
+
+def finish(r, gin, gout, gproj):
+    for t in range(12):
+        gproj[:, t * 128 : (t + 1) * 128] = r[t * 96 : 96 + t * 96]
     for t in range(9):
-        gout[t] = r[t * 96 : (t + 1) * 96, :96]
-    for t in range(12):
-        gproj[:, t * 128 : (t + 1) * 128] = r[864 + t * 96 : 960 + t * 96]
-    for _ in late:
-        pass
-    for t in range(9):
+        gout[t] = r[1152 + t * 96 : 1248 + t * 96, :96]
         gin[t] = r[2048 + t * 96 : 2144 + t * 96, :96]
-    for c in first + second:
-        c.wait_send()
 
 
 def gradients(features, teacher, conv_in, conv_out, projector):
     bf16, f32 = jnp.bfloat16, jnp.float32
     vmem = pl.BlockSpec(memory_space=pltpu.VMEM)
-    hbm = pl.BlockSpec(memory_space=pl.ANY)
-    return pl.pallas_call(
+    hbm = pl.BlockSpec(memory_space=pltpu.HBM)
+    sums = pl.pallas_call(
         main_kernel,
-        out_shape=(
-            jax.ShapeDtypeStruct((9, 96, 96), f32),
-            jax.ShapeDtypeStruct((9, 96, 96), f32),
-            jax.ShapeDtypeStruct((96, 1536), f32),
-        ),
+        out_shape=jax.ShapeDtypeStruct((ROWS, 128), f32),
         in_specs=[hbm] * 5,
-        out_specs=(vmem, vmem, vmem),
+        out_specs=vmem,
         scratch_shapes=[
             pltpu.VMEM((ROWS, 128), f32),
-            pltpu.VMEM((ROWS, 128), f32),
-            pltpu.SemaphoreType.DMA((2, 48)),
-            pltpu.SemaphoreType.DMA((2, 48)),
-            *reduce_scratch(2048),
+            pltpu.SemaphoreType.DMA((3, 48)),
+            pltpu.SemaphoreType.DMA((3, 48)),
+            *reduce_scratch(1024),
+            *reduce_scratch(1024),
             *reduce_scratch(1024),
             pltpu.VMEM((96, 16, 256), bf16),
             pltpu.VMEM((9, 96, 96), bf16),
@@ -456,16 +476,26 @@
             pltpu.VMEM((96, 1824), bf16),
             pltpu.VMEM((1632, 128), f32),
             pltpu.VMEM((864, 128), bf16),
-            pltpu.VMEM((2, 96, 128), bf16),
-            pltpu.VMEM((2, 8, 96, 128), bf16),
+            pltpu.VMEM((2, 128, 128), bf16),
+            pltpu.VMEM((2, 8, 128, 128), bf16),
             pltpu.SemaphoreType.DMA((10,)),
             pltpu.SemaphoreType.DMA((2, 10)),
             pltpu.SemaphoreType.DMA((2, 10)),
         ],
         compiler_params=pltpu.CompilerParams(
-            collective_id=0, has_side_effects=True, vmem_limit_bytes=63 * 2**20
+            collective_id=0, has_side_effects=True, vmem_limit_bytes=62 * 2**20
         ),
     )(features, teacher, conv_in, conv_out, projector)
+    return pl.pallas_call(
+        finish,
+        out_shape=(
+            jax.ShapeDtypeStruct((9, 96, 96), f32),
+            jax.ShapeDtypeStruct((9, 96, 96), f32),
+            jax.ShapeDtypeStruct((96, 1536), f32),
+        ),
+        in_specs=[vmem],
+        out_specs=(vmem, vmem, vmem),
+    )(sums)
 
 
 def solution(mesh):

time: 88 us -> 75.7 us (0.86)
  Pallas kernels: 81.6 us -> 75 us
  local copies, waits for them, and re-layouts: 5.52 us -> 0 us
    pallas_call x1 -> x2, Pallas kernels: 81.6 us -> 75 us  [the longest x1 72.4 us: gradients(): pl.pallas_call(main_kernel, out_shape=jax.ShapeDtypeStruct((ROWS, 128), f...]
    unnamed x3 -> x0, local copies, waits for them, and re-layouts: 5.52 us -> none
where the time goes in v4:
time: 75.7 us; the launch traced here: 75.6 us
  Pallas kernels  75 us (99%)
    pallas_call x1, Pallas kernels, gradients(): pl.pallas_call(main_kernel, out_shape=jax.ShapeDtypeStruct((ROWS, 128), f...  72.4 us
    pallas_call x1, Pallas kernels, gradients(): pl.pallas_call(finish, out_shape=(jax.ShapeDtypeStruct((9, 96, 96), f32),...  2.54 us

profile of v4, /device:TPU:1, one launch (start us, length us, event | category | flops | bytes accessed | tf_op | source)
XLA Modules:
  0.0 75.6 jit_solution(9700662256372784370)
XLA Ops:
  0.6 72.4 %shard_map.76.r = f32[3072,128]{1,0:T(8,128)} custom-call(bf16[96,16,256]{2,1,0:T(8,128)(2,1)} %feat.1, bf16[1536,16,256]{2,1,0:T(8,128)(2,1)} %teach.1, bf16[9,96,96]{2,1,0:T(8,128)(2,1)} %cin.1, bf16[9,96,96]{2,1,0:T(8,128)(2,1)} %cout.1, bf16[96,1536]{1,0:T(8,128)(2,1)} %proj.1), custom_call_target="tpu_custom_call" | custom-call | tf_op jit(solution)/shard_map/pallas_call | solution.py:451
  73.1 2.5 %shard_map.77 = (f32[9,96,96]{2,1,0:T(8,128)}, f32[9,96,96]{2,1,0:T(8,128)}, f32[96,1536]{1,0:T(8,128)}) custom-call(f32[3072,128]{1,0:T(8,128)} %shard_map.76.r), custom_call_target="tpu_custom_call" | custom-call | tf_op jit(solution)/shard_map/pallas_call | solution.py:489

commit v5 on v4

--- a/solution.py
+++ b/solution.py
@@ -24,13 +24,16 @@
     for axis, n in (("x", 4), ("y", 4), ("z", 8)):
         for step in range(1, n):
             yield device(at, **{axis: (at[axis] + step) % n})
+    for axis in "xy":
+        for step in range(1, 4):
+            yield device(at, **{axis: (at[axis] + step) % 4, "core": 1 - at["core"]})
 
 
 def al(x):
     return pl.multiple_of(x, 8)
 
 
-def reduce_rows(at, v, r, base, count, bufs, sent, got):
+def reduce_rows(at, v, r, base, count, bufs, sent, got, short):
     w, in0, in1, in2, out3, in3, sums3 = bufs
     half, colour, big, small, unit = (count // k for k in (2, 4, 16, 64, 256))
     orders = (("x", "y"), ("y", "x"))
@@ -85,23 +88,36 @@
         smalls.append(al(starts[k] + at[axis] * small))
         total = w[pl.ds(smalls[k], small)] + in2[k, 0] + in2[k, 1] + in2[k, 2]
         out3[k * 4 : k * 4 + 4] = total.reshape(4, unit, 128)
-    waits = []
-    for step in range(1, 8):
-        q = (z + step) % 8
-        waits.append(copy(out3.at[q], in3.at[step - 1], device(at, z=q)))
-    yield
-    total = out3[z]
-    for k, c in enumerate(waits):
-        c.wait_recv()
-        total = total + in3[k]
-    sums3[z] = total
-    waits = []
-    for step in range(1, 8):
-        q = (z + step) % 8
-        waits.append(copy(sums3.at[z], sums3.at[z], device(at, z=q)))
-    yield
-    for c in waits:
-        c.wait_recv()
+    if short:
+        in3[z] = out3[...]
+        waits = []
+        for step in range(1, 8):
+            waits.append(copy(out3, in3.at[z], device(at, z=(z + step) % 8)))
+        yield
+        for c in waits:
+            c.wait_recv()
+        total = in3[0]
+        for k in range(1, 8):
+            total = total + in3[k]
+        sums3[...] = total
+    else:
+        waits = []
+        for step in range(1, 8):
+            q = (z + step) % 8
+            waits.append(copy(out3.at[q], in3.at[step - 1], device(at, z=q)))
+        yield
+        total = out3[z]
+        for k, c in enumerate(waits):
+            c.wait_recv()
+            total = total + in3[k]
+        sums3[z] = total
+        waits = []
+        for step in range(1, 8):
+            q = (z + step) % 8
+            waits.append(copy(sums3.at[z], sums3.at[z], device(at, z=q)))
+        yield
+        for c in waits:
+            c.wait_recv()
     waits = []
     for k, axis in enumerate(("y", "x")):
         rows = pl.ds(al(mine + smalls[k]), small)
@@ -120,21 +136,28 @@
             q = (at[axis] + step) % 4
             waits.append(copy(r.at[rows], r.at[rows], device(at, **{axis: q})))
         last.append(copy(r.at[rows], r.at[rows], other))
+        if short:
+            for step in range(1, 4):
+                peer = device(at, **{axis: (at[axis] + step) % 4, "core": 1 - core})
+                last.append(copy(r.at[rows], r.at[rows], peer))
     yield
-    for k, axis in enumerate(("x", "y")):
+    if short:
+        last += waits
+    for k, axis in enumerate(() if short else ("x", "y")):
         for step in range(1, 4):
             q = (at[axis] - step + 4) % 4
             rows = pl.ds(al(mine + k * colour + q * big), big)
             waits[3 * k + step - 1].wait_recv()
             last.append(copy(r.at[rows], r.at[rows], other))
-    yield
+    if not short:
+        yield
     for c in last:
         c.wait_recv()
     for c in copies:
         c.wait_send()
 
 
-def reduce_scratch(count):
+def reduce_scratch(count, short):
     half, colour, big, small, unit = (count // k for k in (2, 4, 16, 64, 256))
     f32 = jnp.float32
     return [
@@ -143,7 +166,7 @@
         pltpu.VMEM((2, 3, big, 128), f32),
         pltpu.VMEM((2, 3, small, 128), f32),
         pltpu.VMEM((8, unit, 128), f32),
-        pltpu.VMEM((7, unit, 128), f32),
+        pltpu.VMEM((8, 8, unit, 128) if short else (7, unit, 128), f32),
         pltpu.VMEM((8, unit, 128), f32),
     ]
 
@@ -353,7 +376,7 @@
         taps[t * 96 : (t + 1) * 96] = pltpu.roll(edge, (128 - away) % 128, 1).astype(bf16)
     pre = dot(w1[...], taps[...])
     side = jnp.where(off, 0.0, (pre * phi(pre)).astype(bf16).astype(f32))
-    shifted(hh, 0, 18, 1, side)
+    shifted(hh, 0, 4, 1, side)
 
     def conv2(h, _):
         s = (xh[h + 2, 1].astype(f32) + dot(w2[...], window(hh, h))).astype(bf16)
@@ -362,7 +385,16 @@
         ds[h + 1, 1] = (dot(lhs[...], t2[h]) * SCALE).astype(bf16)
         return 0
 
-    lax.fori_loop(0, 16, conv2, 0, unroll=2)
+    def conv2_pair(i, _):
+        for k in range(2):
+            conv2(i * 2 + k, 0)
+        for k in range(2):
+            shift_row(hh, i * 2 + 4 + k, 1, side)
+        return 0
+
+    lax.fori_loop(0, 7, conv2_pair, 0)
+    for h in (14, 15):
+        conv2(h, 0)
     tile[1] = own_tile(lambda h: ds[h + 1, 1])
     second_sides, second = exchange(1, ds.at[1, 1], ds.at[16, 1], ds.at[0, 1], ds.at[17, 1])
 
@@ -386,7 +418,7 @@
         v[k * 96 : 96 + k * 96] = (mp[:, part] - gacc[part].T[:96]) * SCALE
     sums = {
         name: reduce_rows(
-            place_here, v, r, k * 1024, 1024, bufs, sent_sum.at[k], got_sum.at[k]
+            place_here, v, r, k * 1024, 1024, bufs, sent_sum.at[k], got_sum.at[k], name != "E"
         )
         for k, (name, bufs) in enumerate(
             (
@@ -409,7 +441,8 @@
     def _():
         ds[17, 1] = jnp.zeros((96, 256), bf16)
 
-    shifted(ds, 0, 18, 1, rim(1, True))
+    edge2 = rim(1, True)
+    shifted(ds, 0, 6, 1, edge2)
 
     def back(h, _):
         def dpre(k):
@@ -419,13 +452,20 @@
         return 0
 
     next(sums["E"])
-    lax.fori_loop(0, 4, back, 0)
+    def back_next(i, _):
+        back(i, 0)
+        for k in range(4):
+            shift_row(ds, i * 4 + 6 + k, 1, edge2)
+        return 0
+
+    lax.fori_loop(0, 3, back_next, 0)
+    back(3, 0)
     next(sums["L"])
     next(sums["E"])
     lax.fori_loop(0, 2, grads_out, 0)
     next(sums["L"])
     lax.fori_loop(2, 4, grads_out, 0)
-    for name in "MEMLEMLMELEMLEMLEM":
+    for name in "MEMLEMLMELEMLEM":
         next(sums[name], None)
     for _ in sums["L"]:
         pass
@@ -457,9 +497,9 @@
             pltpu.VMEM((ROWS, 128), f32),
             pltpu.SemaphoreType.DMA((3, 48)),
             pltpu.SemaphoreType.DMA((3, 48)),
-            *reduce_scratch(1024),
-            *reduce_scratch(1024),
-            *reduce_scratch(1024),
+            *reduce_scratch(1024, False),
+            *reduce_scratch(1024, True),
+            *reduce_scratch(1024, True),
             pltpu.VMEM((96, 16, 256), bf16),
             pltpu.VMEM((9, 96, 96), bf16),
             pltpu.VMEM((9, 96, 96), bf16),

time: 75.7 us -> 69.4 us (0.917)
  Pallas kernels: 75 us -> 68.6 us
    pallas_call x1, Pallas kernels: 72.4 us -> 66.1 us  [gradients(): pl.pallas_call(main_kernel, out_shape=jax.ShapeDtypeStruct((ROWS, 128), f...]
where the time goes in v5:
time: 69.4 us; the launch traced here: 69.3 us
  Pallas kernels  68.6 us (99%)
    pallas_call x1, Pallas kernels, gradients(): pl.pallas_call(main_kernel, out_shape=jax.ShapeDtypeStruct((ROWS, 128), f...  66.1 us
    pallas_call x1, Pallas kernels, gradients(): pl.pallas_call(finish, out_shape=(jax.ShapeDtypeStruct((9, 96, 96), f32),...  2.54 us

profile of v5, /device:TPU:1, one launch (start us, length us, event | category | flops | bytes accessed | tf_op | source)
XLA Modules:
  0.0 69.3 jit_solution(9916456686125785644)
XLA Ops:
  0.6 66.1 %shard_map.76.r = f32[3072,128]{1,0:T(8,128)} custom-call(bf16[96,16,256]{2,1,0:T(8,128)(2,1)} %feat.1, bf16[1536,16,256]{2,1,0:T(8,128)(2,1)} %teach.1, bf16[9,96,96]{2,1,0:T(8,128)(2,1)} %cin.1, bf16[9,96,96]{2,1,0:T(8,128)(2,1)} %cout.1, bf16[96,1536]{1,0:T(8,128)(2,1)} %proj.1), custom_call_target="tpu_custom_call" | custom-call | tf_op jit(solution)/shard_map/pallas_call | solution.py:491
  66.7 2.5 %shard_map.77 = (f32[9,96,96]{2,1,0:T(8,128)}, f32[9,96,96]{2,1,0:T(8,128)}, f32[96,1536]{1,0:T(8,128)}) custom-call(f32[3072,128]{1,0:T(8,128)} %shard_map.76.r), custom_call_target="tpu_custom_call" | custom-call | tf_op jit(solution)/shard_map/pallas_call | solution.py:529
